TPU v7x, 32 devices: a whole 2x2x4 slice. The times are simulated.
32 devices in a mesh: grp: 2 (over x), seq: 16 (over z, y, core).
Axes of the slice: x: 2, y: 2, z: 4, core: 2. Of those that a mesh axis runs over, the one named last changes fastest.
Arguments:
- queries: bfloat16 [128, 5120], P(('grp', 'seq')), parts along dimension 0
- keys: bfloat16 [16384, 5120], P(('grp', 'seq')), parts along dimension 0
- values: bfloat16 [16384, 5120], P(('grp', 'seq')), parts along dimension 0, may hold values from -6 to 6
- gain: float32 [5120], replicated, may hold values from 0.1 to 1.9
Outputs:
- window_out: bfloat16 [128, 5120], P(('grp', 'seq')), parts along dimension 0
There are 2 independent parts, one for each index of `grp`. A program takes and returns all parts, laid end to end along the dimension named above; an argument that names none is the same for every part. Nothing has to cross between parts.
All inputs are finite; a program needn't handle non-finite values.
Results may differ from a plain program's by a relative error of at most 0.001.
Values may be sent and summed in bfloat16 or wider, within the bound.
No kernel may reach another device: no remote copies, remote signals or barrier semaphores. Data moves between devices by JAX's collectives and lax.ppermute only.
A program may use at most 128 MiB of HBM per device.

v0:
```python
import functools
import math

import jax
import jax.numpy as jnp
from jax import lax
from jax.experimental import pallas as pl
from jax.experimental.pallas import tpu as pltpu
from jax.sharding import PartitionSpec as P

HDIM = 128
EXP2_SCALE = math.log2(math.e) / math.sqrt(HDIM)
FETCH_FLOPS = 1_500_000_000
CODE_SPAN = 250.0
VMEM_SPEC = pl.BlockSpec(memory_space=pltpu.VMEM)


def copy_kernel(source_ref, out_ref):
    out_ref[...] = source_ref[...]


def join_kernel(here_ref, there_ref, out_ref):
    out_ref[...] = jnp.concatenate([here_ref[...], there_ref[...]], axis=0)


def attend_kernel(query_here_ref, query_there_ref, key_ref, value_ref, keep_ref, send_ref, dots_ref, weights_ref):
    half, width = query_here_ref.shape
    rows = 2 * half
    heads = width // HDIM
    slots = dots_ref.shape[0]

    def score(head):
        columns = slice(head * HDIM, (head + 1) * HDIM)
        dots_ref[head % slots] = lax.dot_general(
            jnp.concatenate([query_here_ref[:, columns], query_there_ref[:, columns]], axis=0),
            key_ref[:, columns],
            (((1,), (1,)), ((), ())),
            preferred_element_type=jnp.float32,
        )

    def weigh(head):
        dots = dots_ref[head % slots]
        peak = jnp.max(dots, axis=1, keepdims=True)
        weights = jnp.exp2((dots - peak) * EXP2_SCALE)
        total = jnp.sum(weights, axis=1, keepdims=True)
        coarse = weights.astype(jnp.bfloat16)
        weights_ref[head % slots, :rows] = coarse
        weights_ref[head % slots, rows:] = (weights - coarse.astype(jnp.float32)).astype(jnp.bfloat16)
        for ref, first in ((keep_ref, 0), (send_ref, half)):
            ref[:, width + head : width + head + 1] = peak[first : first + half]
            ref[:, width + HDIM + head : width + HDIM + head + 1] = total[first : first + half]

    def accumulate(head):
        columns = slice(head * HDIM, (head + 1) * HDIM)
        sums = jnp.dot(weights_ref[head % slots], value_ref[:, columns], preferred_element_type=jnp.float32)
        numerator = sums[:rows] + sums[rows:]
        keep_ref[:, columns] = numerator[:half]
        send_ref[:, columns] = numerator[half:]

    group = slots // 2
    for ref in (keep_ref, send_ref):
        ref[:, width:] = jnp.zeros((half, 2 * HDIM), jnp.float32)
    steps = heads // group
    for step in range(steps + 2):
        for member in range(group):
            for stage, lag in ((score, 0), (weigh, 1), (accumulate, 2)):
                if 0 <= step - lag < steps:
                    stage((step - lag) * group + member)


def pack_exact(values, heads):
    lane = lax.broadcasted_iota(jnp.int32, values.shape, 1)
    first = values.astype(jnp.bfloat16).astype(jnp.float32)
    rest = values - first
    second = rest.astype(jnp.bfloat16).astype(jnp.float32)
    third = rest - second
    tail = jnp.where(lane < 2 * heads, pltpu.roll(second, heads, 1), pltpu.roll(third, 2 * heads, 1))
    return jnp.where(lane < heads, first, tail).astype(jnp.bfloat16)


def unpack_exact(packed, heads):
    terms = packed.astype(jnp.float32)
    return terms + (pltpu.roll(terms, HDIM - heads, 1) + pltpu.roll(terms, HDIM - 2 * heads, 1))


def read_statistics(ref, width, coded):
    if not coded:
        return ref[:, width : width + HDIM], ref[:, width + HDIM :], None
    heads = width // HDIM
    maxima = unpack_exact(ref[:, width : width + HDIM], heads)
    denominators = unpack_exact(ref[:, width + HDIM : width + 2 * HDIM], heads)
    return maxima, denominators, ref[:, width + 2 * HDIM :].astype(jnp.float32) * (1.0 / CODE_SPAN)


def read_numerator(ref, columns, coded):
    if not coded:
        return ref[:, columns]
    code = ref[:, columns].astype(jnp.float32)
    size = jnp.log2(jnp.abs(code)) + CODE_SPAN / 2
    return jnp.where(code < 0, -size, size)


def combine(refs, coded, width):
    statistics = [read_statistics(ref, width, c) for ref, c in zip(refs, coded)]
    maxima = functools.reduce(jnp.maximum, [m for m, _, _ in statistics])
    scales = [jnp.exp2((m - maxima) * EXP2_SCALE) for m, _, _ in statistics]
    denominators = sum(scale * d for scale, (_, d, _) in zip(scales, statistics))
    factors = [scale if unit is None else scale * unit for scale, (_, _, unit) in zip(scales, statistics)]
    return maxima, denominators, factors


def combined_numerator(refs, coded, factors, head):
    columns = slice(head * HDIM, (head + 1) * HDIM)
    lane = slice(head, head + 1)
    return sum(f[:, lane] * read_numerator(ref, columns, c) for ref, c, f in zip(refs, coded, factors))


def merge_kernel(here_ref, there_ref, keep_ref, send_ref, *, coded):
    sources = (here_ref, there_ref)
    half, padded = keep_ref.shape
    width = padded - 2 * HDIM
    heads = width // HDIM
    maxima, denominators, factors = combine(sources, coded, width)
    lane = lax.broadcasted_iota(jnp.int32, (half, HDIM), 1)
    units = jnp.ones((half, HDIM), jnp.float32)
    for head in range(heads):
        columns = slice(head * HDIM, (head + 1) * HDIM)
        merged = combined_numerator(sources, coded, factors, head)
        keep_ref[:, columns] = merged[:half]
        merged = merged[half:]
        size = jnp.abs(merged)
        largest = jnp.maximum(jnp.max(size, axis=1, keepdims=True), 1e-30)
        unit = (largest * 1.01).astype(jnp.bfloat16).astype(jnp.float32)
        code = jnp.exp2(size * (CODE_SPAN / unit) - CODE_SPAN / 2)
        send_ref[:, columns] = jnp.where(merged < 0, -code, code).astype(jnp.bfloat16)
        units = jnp.where(lane == head, unit, units)
    keep_ref[:, width : width + HDIM] = maxima[:half]
    keep_ref[:, width + HDIM :] = denominators[:half]
    send_ref[:, width : width + HDIM] = pack_exact(maxima[half:], heads)
    send_ref[:, width + HDIM : width + 2 * HDIM] = pack_exact(denominators[half:], heads)
    send_ref[:, width + 2 * HDIM :] = units.astype(jnp.bfloat16)


def finish_kernel(here_ref, there_ref, gain_ref, out_ref, *, coded):
    sources = (here_ref, there_ref)
    rows, width = out_ref.shape
    _, denominators, factors = combine(sources, coded, width)
    factors = [factor / denominators for factor in factors]
    squares = jnp.zeros((rows, HDIM), jnp.float32)
    attended = []
    for head in range(width // HDIM):
        block = combined_numerator(sources, coded, factors, head)
        squares = squares + block * block
        attended.append(block)
    mean = jnp.sum(squares, axis=1, keepdims=True) / width
    inverse = 1.0 / jnp.sqrt(mean + 1e-06)
    for head, block in enumerate(attended):
        columns = slice(head * HDIM, (head + 1) * HDIM)
        out_ref[:, columns] = (block * inverse * gain_ref[:, columns]).astype(out_ref.dtype)


def call(kernel, out_shape, operands, flops=0, scratch=(), limit=4 << 20):
    outs = out_shape if isinstance(out_shape, (tuple, list)) else [out_shape]
    size = sum(math.prod(a.shape) * a.dtype.itemsize for a in (*operands, *outs))
    return pl.pallas_call(
        kernel,
        out_shape=out_shape,
        in_specs=[VMEM_SPEC] * len(operands),
        out_specs=jax.tree.map(lambda _: VMEM_SPEC, out_shape),
        scratch_shapes=scratch,
        cost_estimate=pl.CostEstimate(flops=flops, bytes_accessed=size, transcendentals=0),
        compiler_params=pltpu.CompilerParams(vmem_limit_bytes=limit),
    )(*operands)


def exchange(array, masks):
    return lax.ppermute(array, "seq", [(i, i ^ masks[i % 2]) for i in range(lax.axis_size("seq"))])


def chip_stages(peers):
    first = [1 << bit for bit in range(1, peers.bit_length() - 1)]
    second = [*first[1::-1], *first[2:]]
    return list(zip(first, second))


def shards(queries, keys, values, gain):
    stages = chip_stages(lax.axis_size("seq"))
    cores = (1, 1)
    rows, width = queries.shape
    tokens = keys.shape[0]
    gain = call(copy_kernel, jax.ShapeDtypeStruct((1, width), gain.dtype), [gain.reshape(1, width)], FETCH_FLOPS)
    window = queries
    for masks in reversed(stages):
        arrived = exchange(window, masks)
        both = jax.ShapeDtypeStruct((2 * window.shape[0], width), window.dtype)
        window = call(join_kernel, both, [window, arrived], FETCH_FLOPS)
    arrived = exchange(window, cores)
    half = window.shape[0]

    plain = lambda count: jax.ShapeDtypeStruct((count, width + 2 * HDIM), jnp.float32)
    code = lambda count: jax.ShapeDtypeStruct((count, width + 3 * HDIM), jnp.bfloat16)
    keep, send = call(
        attend_kernel,
        (plain(half), plain(half)),
        (window, arrived, keys, values),
        8 * half * tokens * width,
        [pltpu.VMEM((4, 2 * half, tokens), jnp.float32), pltpu.VMEM((4, 4 * half, tokens), jnp.bfloat16)],
        16 << 20,
    )
    sources, coded = (keep, exchange(send, cores)), (False, False)
    for masks in stages:
        half = half // 2
        kernel = functools.partial(merge_kernel, coded=coded)
        keep, send = call(kernel, (plain(half), code(half)), sources, 0)
        sources, coded = (keep, exchange(send, masks)), (False, True)
    out = jax.ShapeDtypeStruct((rows, width), jnp.bfloat16)
    return call(functools.partial(finish_kernel, coded=coded), out, (*sources, gain), 0)


def solution(mesh):
    spec = P(("grp", "seq"), None)
    return jax.shard_map(shards, mesh=mesh, in_specs=(spec, spec, spec, P()), out_specs=spec, check_vma=False)
```

profile of v0, /device:TPU:0, one launch (start us, length us, event | category | flops | bytes accessed | tf_op | source)
XLA Modules:
  0.0 48.1 jit_solution(8153023326738204151)
XLA Ops:
  0.0 4.1 %collective-permute-start = (bf16[4,5120]{1,0:T(4,128)(2,1)}, bf16[4,5120]{1,0:T(4,128)(2,1)S(1)}, u32[]{:S(2)}, u32[]{:S(2)}) collective-permute-start(bf16[4,5120]{1,0:T(4,128)(2,1)} %here_ref.1), channel_id=1, source_target_pairs={{0,8},{1,9},{2,10},{3,11},{4,12},{5,13},{6,14},{7,15},{8,0},{9,1},... | collective-permute-start | bytes 122888 | tf_op jit(solution)/shard_map/ppermute | solution.py:177
  4.1 2.6 %collective-permute-done.there_ref = bf16[4,5120]{1,0:T(4,128)(2,1)S(1)} collective-permute-done((bf16[4,5120]{1,0:T(4,128)(2,1)}, bf16[4,5120]{1,0:T(4,128)(2,1)S(1)}, u32[]{:S(2)}, u32[]{:S(2)}) %collective-permute-start) | collective-permute-done | bytes 40992 | tf_op jit(solution)/shard_map/ppermute | solution.py:177
  6.7 0.8 %copy-done = bf16[4,5120]{1,0:T(4,128)(2,1)S(1)} copy-done((bf16[4,5120]{1,0:T(4,128)(2,1)S(1)}, bf16[4,5120]{1,0:T(4,128)(2,1)}, u32[]{:S(2)}) %copy-start) | copy-done | bytes 40984
  7.5 0.0 slice-start.1
  7.5 0.0 slice-start.3
  7.5 1.5 %collective-permute-start.1 = (bf16[8,5120]{1,0:T(8,128)(2,1)S(1)}, bf16[8,5120]{1,0:T(8,128)(2,1)S(1)}, u32[]{:S(2)}, u32[]{:S(2)}) collective-permute-start(bf16[8,5120]{1,0:T(8,128)(2,1)S(1)} %shard_map.46.here_ref), channel_id=1, source_target_pairs={{0,4},{1,3},{2,6},{3,1},{4,0},{5,7},{6,2},{7,5},{8,12},{9,11},{10,... | collective-permute-start | bytes 245768 | tf_op jit(solution)/shard_map/ppermute | solution.py:177
  9.1 3.0 %collective-permute-done.1.there_ref = bf16[8,5120]{1,0:T(8,128)(2,1)S(1)} collective-permute-done((bf16[8,5120]{1,0:T(8,128)(2,1)S(1)}, bf16[8,5120]{1,0:T(8,128)(2,1)S(1)}, u32[]{:S(2)}, u32[]{:S(2)}) %collective-permute-start.1) | collective-permute-done | bytes 81952 | tf_op jit(solution)/shard_map/ppermute | solution.py:177
  12.1 1.9 %collective-permute-start.2 = (bf16[16,5120]{1,0:T(8,128)(2,1)S(1)}, bf16[16,5120]{1,0:T(8,128)(2,1)S(1)}, u32[]{:S(2)}, u32[]{:S(2)}) collective-permute-start(bf16[16,5120]{1,0:T(8,128)(2,1)S(1)} %shard_map.47.here_ref), channel_id=1, source_target_pairs={{0,2},{1,5},{2,0},{3,7},{4,6},{5,1},{6,4},{7,3},{8,10},{9,13},{10,... | collective-permute-start | bytes 491528 | tf_op jit(solution)/shard_map/ppermute | solution.py:177
  14.0 3.5 %collective-permute-done.2.there_ref = bf16[16,5120]{1,0:T(8,128)(2,1)S(1)} collective-permute-done((bf16[16,5120]{1,0:T(8,128)(2,1)S(1)}, bf16[16,5120]{1,0:T(8,128)(2,1)S(1)}, u32[]{:S(2)}, u32[]{:S(2)}) %collective-permute-start.2) | collective-permute-done | bytes 163872 | tf_op jit(solution)/shard_map/ppermute | solution.py:177
  17.5 0.1 collective-permute-start.3
  17.6 1.6 %collective-permute-done.3.query_there_ref = bf16[32,5120]{1,0:T(8,128)(2,1)S(1)} collective-permute-done((bf16[32,5120]{1,0:T(8,128)(2,1)S(1)}, bf16[32,5120]{1,0:T(8,128)(2,1)S(1)}, u32[]{:S(2)}, u32[]{:S(2)}) %collective-permute-start.3) | collective-permute-done | bytes 327712 | tf_op jit(solution)/shard_map/ppermute | solution.py:177
  19.2 3.6 %shard_map.49 = (f32[32,5376]{1,0:T(8,128)S(1)}, f32[32,5376]{1,0:T(8,128)S(1)}) custom-call(bf16[32,5120]{1,0:T(8,128)(2,1)S(1)} %shard_map.48.query_here_ref, bf16[32,5120]{1,0:T(8,128)(2,1)S(1)} %collective-permute-done.3.query_there_ref, bf16[512,5120]{1,0:T(8,128)(2,1)S(1)} %bitcast.2, bf16[512,5120]{1,0:T(8,128)(2,1)S(1)} %bitcast.4), custom_call_target="tpu_custom_call" | custom-call | flops 671088640 | bytes 12517376 | tf_op jit(solution)/shard_map/pallas_call | solution.py:165
  22.8 0.2 collective-permute-start.4
  23.0 2.0 %collective-permute-done.4.there_ref = f32[32,5376]{1,0:T(8,128)S(1)} collective-permute-done((f32[32,5376]{1,0:T(8,128)S(1)}, f32[32,5376]{1,0:T(8,128)S(1)}, u32[]{:S(2)}, u32[]{:S(2)}) %collective-permute-start.4) | collective-permute-done | bytes 688160 | tf_op jit(solution)/shard_map/ppermute | solution.py:177
  25.0 3.5 %shard_map.50 = (f32[16,5376]{1,0:T(8,128)S(1)}, bf16[16,5504]{1,0:T(8,128)(2,1)S(1)}) custom-call(f32[32,5376]{1,0:T(8,128)S(1)} %get-tuple-element.13.here_ref, f32[32,5376]{1,0:T(8,128)S(1)} %collective-permute-done.4.there_ref), custom_call_target="tpu_custom_call" | custom-call | bytes 1896448 | tf_op jit(solution)/shard_map/pallas_call | solution.py:165
  28.6 1.9 %collective-permute-start.5 = (bf16[16,5504]{1,0:T(8,128)(2,1)S(1)}, bf16[16,5504]{1,0:T(8,128)(2,1)S(1)}, u32[]{:S(2)}, u32[]{:S(2)}) collective-permute-start(bf16[16,5504]{1,0:T(8,128)(2,1)S(1)} %get-tuple-element.16), channel_id=1, source_target_pairs={{0,2},{1,5},{2,0},{3,7},{4,6},{5,1},{6,4},{7,3},{8,10},{9,13},{10,... | collective-permute-start | bytes 528392 | tf_op jit(solution)/shard_map/ppermute | solution.py:177
  30.4 3.6 %collective-permute-done.5.there_ref = bf16[16,5504]{1,0:T(8,128)(2,1)S(1)} collective-permute-done((bf16[16,5504]{1,0:T(8,128)(2,1)S(1)}, bf16[16,5504]{1,0:T(8,128)(2,1)S(1)}, u32[]{:S(2)}, u32[]{:S(2)}) %collective-permute-start.5) | collective-permute-done | bytes 176160 | tf_op jit(solution)/shard_map/ppermute | solution.py:177
  34.1 1.7 %shard_map.51 = (f32[8,5376]{1,0:T(8,128)S(1)}, bf16[8,5504]{1,0:T(8,128)(2,1)S(1)}) custom-call(f32[16,5376]{1,0:T(8,128)S(1)} %get-tuple-element.15.here_ref, bf16[16,5504]{1,0:T(8,128)(2,1)S(1)} %collective-permute-done.5.there_ref), custom_call_target="tpu_custom_call" | custom-call | bytes 780288 | tf_op jit(solution)/shard_map/pallas_call | solution.py:165
  35.7 1.5 %collective-permute-start.6 = (bf16[8,5504]{1,0:T(8,128)(2,1)S(1)}, bf16[8,5504]{1,0:T(8,128)(2,1)S(1)}, u32[]{:S(2)}, u32[]{:S(2)}) collective-permute-start(bf16[8,5504]{1,0:T(8,128)(2,1)S(1)} %get-tuple-element.18), channel_id=1, source_target_pairs={{0,4},{1,3},{2,6},{3,1},{4,0},{5,7},{6,2},{7,5},{8,12},{9,11},{10,... | collective-permute-start | bytes 264200 | tf_op jit(solution)/shard_map/ppermute | solution.py:177
  37.3 3.0 %collective-permute-done.6.there_ref = bf16[8,5504]{1,0:T(8,128)(2,1)S(1)} collective-permute-done((bf16[8,5504]{1,0:T(8,128)(2,1)S(1)}, bf16[8,5504]{1,0:T(8,128)(2,1)S(1)}, u32[]{:S(2)}, u32[]{:S(2)}) %collective-permute-start.6) | collective-permute-done | bytes 88096 | tf_op jit(solution)/shard_map/ppermute | solution.py:177
  40.3 1.8 %shard_map.52 = (f32[4,5376]{1,0:T(4,128)S(1)}, bf16[4,5504]{1,0:T(4,128)(2,1)S(1)}) custom-call(f32[8,5376]{1,0:T(8,128)S(1)} %get-tuple-element.17.here_ref, bf16[8,5504]{1,0:T(8,128)(2,1)S(1)} %collective-permute-done.6.there_ref), custom_call_target="tpu_custom_call" | custom-call | bytes 390144 | tf_op jit(solution)/shard_map/pallas_call | solution.py:165
  42.1 2.6 %collective-permute-start.7 = (bf16[4,5504]{1,0:T(4,128)(2,1)S(1)}, bf16[4,5504]{1,0:T(4,128)(2,1)S(1)}, u32[]{:S(2)}, u32[]{:S(2)}) collective-permute-start(bf16[4,5504]{1,0:T(4,128)(2,1)S(1)} %get-tuple-element.20), channel_id=1, source_target_pairs={{0,8},{1,9},{2,10},{3,11},{4,12},{5,13},{6,14},{7,15},{8,0},{9,1},... | collective-permute-start | bytes 132104 | tf_op jit(solution)/shard_map/ppermute | solution.py:177
  44.7 2.4 %collective-permute-done.7.there_ref = bf16[4,5504]{1,0:T(4,128)(2,1)S(1)} collective-permute-done((bf16[4,5504]{1,0:T(4,128)(2,1)S(1)}, bf16[4,5504]{1,0:T(4,128)(2,1)S(1)}, u32[]{:S(2)}, u32[]{:S(2)}) %collective-permute-start.7) | collective-permute-done | bytes 44064 | tf_op jit(solution)/shard_map/ppermute | solution.py:177
  47.1 1.0 %shard_map.54 = bf16[4,5120]{1,0:T(4,128)(2,1)} custom-call(f32[4,5376]{1,0:T(4,128)S(1)} %get-tuple-element.19.here_ref, bf16[4,5504]{1,0:T(4,128)(2,1)S(1)} %collective-permute-done.7.there_ref, f32[1,5120]{1,0:T(1,128)S(1)} %shard_map.53.gain_ref), custom_call_target="tpu_custom_call" | custom-call | bytes 191488 | tf_op jit(solution)/shard_map/pallas_call | solution.py:165
  (15 shorter events, 0.1 us)
Async XLA Ops:
  0.0 6.7 %collective-permute-start = (bf16[4,5120]{1,0:T(4,128)(2,1)}, bf16[4,5120]{1,0:T(4,128)(2,1)S(1)}, u32[]{:S(2)}, u32[]{:S(2)}) collective-permute-start(bf16[4,5120]{1,0:T(4,128)(2,1)} %here_ref.1), channel_id=1, source_target_pairs={{0,8},{1,9},{2,10},{3,11},{4,12},{5,13},{6,14},{7,15},{8,0},{9,1},... | collective-permute-start | bytes 122888 | tf_op jit(solution)/shard_map/ppermute | solution.py:177
  6.7 0.8 %copy-start = (bf16[4,5120]{1,0:T(4,128)(2,1)S(1)}, bf16[4,5120]{1,0:T(4,128)(2,1)}, u32[]{:S(2)}) copy-start(bf16[4,5120]{1,0:T(4,128)(2,1)} %here_ref.1) | copy-start | bytes 122884
  7.5 11.7 %slice-start = ((s8[5242880]{0:T(1024)(128)(4,1)}), s8[4194304]{0:T(1024)(128)(4,1)S(1)}, s32[]{:S(2)}) async-start(s8[5242880]{0:T(1024)(128)(4,1)} %bitcast.1), calls=%async_computation | async-start | bytes 8388608
  7.5 11.7 %slice-start.2 = ((s8[5242880]{0:T(1024)(128)(4,1)}), s8[4194304]{0:T(1024)(128)(4,1)S(1)}, s32[]{:S(2)}) async-start(s8[5242880]{0:T(1024)(128)(4,1)} %bitcast.3), calls=%async_computation.2 | async-start | bytes 8388608
  7.5 11.7 %slice-start.1 = ((s8[5242880]{0:T(1024)(128)(4,1)}), s8[1048576]{0:T(1024)(128)(4,1)S(1)}, s32[]{:S(2)}) async-start(s8[5242880]{0:T(1024)(128)(4,1)} %bitcast.1), calls=%async_computation.1 | async-start | bytes 2097152
  7.5 11.7 %slice-start.3 = ((s8[5242880]{0:T(1024)(128)(4,1)}), s8[1048576]{0:T(1024)(128)(4,1)S(1)}, s32[]{:S(2)}) async-start(s8[5242880]{0:T(1024)(128)(4,1)} %bitcast.3), calls=%async_computation.3 | async-start | bytes 2097152
  7.5 4.5 %collective-permute-start.1 = (bf16[8,5120]{1,0:T(8,128)(2,1)S(1)}, bf16[8,5120]{1,0:T(8,128)(2,1)S(1)}, u32[]{:S(2)}, u32[]{:S(2)}) collective-permute-start(bf16[8,5120]{1,0:T(8,128)(2,1)S(1)} %shard_map.46.here_ref), channel_id=1, source_target_pairs={{0,4},{1,3},{2,6},{3,1},{4,0},{5,7},{6,2},{7,5},{8,12},{9,11},{10,... | collective-permute-start | bytes 245768 | tf_op jit(solution)/shard_map/ppermute | solution.py:177
  12.1 5.4 %collective-permute-start.2 = (bf16[16,5120]{1,0:T(8,128)(2,1)S(1)}, bf16[16,5120]{1,0:T(8,128)(2,1)S(1)}, u32[]{:S(2)}, u32[]{:S(2)}) collective-permute-start(bf16[16,5120]{1,0:T(8,128)(2,1)S(1)} %shard_map.47.here_ref), channel_id=1, source_target_pairs={{0,2},{1,5},{2,0},{3,7},{4,6},{5,1},{6,4},{7,3},{8,10},{9,13},{10,... | collective-permute-start | bytes 491528 | tf_op jit(solution)/shard_map/ppermute | solution.py:177
  17.5 27.2 %copy-start.1 = (f32[5120]{0:T(1024)S(1)}, f32[5120]{0:T(1024)}, u32[]{:S(2)}) copy-start(f32[5120]{0:T(1024)} %param.7) | copy-start | bytes 61444
  17.5 1.7 %collective-permute-start.3 = (bf16[32,5120]{1,0:T(8,128)(2,1)S(1)}, bf16[32,5120]{1,0:T(8,128)(2,1)S(1)}, u32[]{:S(2)}, u32[]{:S(2)}) collective-permute-start(bf16[32,5120]{1,0:T(8,128)(2,1)S(1)} %shard_map.48.query_here_ref), channel_id=1, source_target_pairs={{0,1},{1,0},{2,3},{3,2},{4,5},{5,4},{6,7},{7,6},{8,9},{9,8},{10,11... | collective-permute-start | bytes 983048 | tf_op jit(solution)/shard_map/ppermute | solution.py:177
  22.8 2.2 %collective-permute-start.4 = (f32[32,5376]{1,0:T(8,128)S(1)}, f32[32,5376]{1,0:T(8,128)S(1)}, u32[]{:S(2)}, u32[]{:S(2)}) collective-permute-start(f32[32,5376]{1,0:T(8,128)S(1)} %get-tuple-element.14), channel_id=1, source_target_pairs={{0,1},{1,0},{2,3},{3,2},{4,5},{5,4},{6,7},{7,6},{8,9},{9,8},{10,11... | collective-permute-start | bytes 2064392 | tf_op jit(solution)/shard_map/ppermute | solution.py:177
  28.6 5.5 %collective-permute-start.5 = (bf16[16,5504]{1,0:T(8,128)(2,1)S(1)}, bf16[16,5504]{1,0:T(8,128)(2,1)S(1)}, u32[]{:S(2)}, u32[]{:S(2)}) collective-permute-start(bf16[16,5504]{1,0:T(8,128)(2,1)S(1)} %get-tuple-element.16), channel_id=1, source_target_pairs={{0,2},{1,5},{2,0},{3,7},{4,6},{5,1},{6,4},{7,3},{8,10},{9,13},{10,... | collective-permute-start | bytes 528392 | tf_op jit(solution)/shard_map/ppermute | solution.py:177
  35.7 4.6 %collective-permute-start.6 = (bf16[8,5504]{1,0:T(8,128)(2,1)S(1)}, bf16[8,5504]{1,0:T(8,128)(2,1)S(1)}, u32[]{:S(2)}, u32[]{:S(2)}) collective-permute-start(bf16[8,5504]{1,0:T(8,128)(2,1)S(1)} %get-tuple-element.18), channel_id=1, source_target_pairs={{0,4},{1,3},{2,6},{3,1},{4,0},{5,7},{6,2},{7,5},{8,12},{9,11},{10,... | collective-permute-start | bytes 264200 | tf_op jit(solution)/shard_map/ppermute | solution.py:177
  42.1 5.0 %collective-permute-start.7 = (bf16[4,5504]{1,0:T(4,128)(2,1)S(1)}, bf16[4,5504]{1,0:T(4,128)(2,1)S(1)}, u32[]{:S(2)}, u32[]{:S(2)}) collective-permute-start(bf16[4,5504]{1,0:T(4,128)(2,1)S(1)} %get-tuple-element.20), channel_id=1, source_target_pairs={{0,8},{1,9},{2,10},{3,11},{4,12},{5,13},{6,14},{7,15},{8,0},{9,1},... | collective-permute-start | bytes 132104 | tf_op jit(solution)/shard_map/ppermute | solution.py:177
where the time goes:
time: 48.3 us; the launch traced here: 48.1 us
  waiting for transfers between devices  21.8 us (45%)
  starting transfers between devices  13.8 us (29%)
  Pallas kernels  11.7 us (24%)
  local copies, waits for them, and re-layouts  0.81 us (2%)
    ppermute x8, waiting for transfers between devices, exchange(): lax.ppermute(array, 'seq', [(i, i ^ masks[i % 2]) for i in range(lax.axis...  21.8 us
    ppermute x8, starting transfers between devices, exchange(): lax.ppermute(array, 'seq', [(i, i ^ masks[i % 2]) for i in range(lax.axis...  13.8 us
    pallas_call x9, Pallas kernels, call(): pl.pallas_call(kernel, out_shape=out_shape, in_specs=[VMEM_SPEC] * len(op...  11.7 us
  transfers between devices with their start and end apart: 8, of which 8 were waited for; matrix products, arithmetic and copies ran while one was open for 0% of the time, Pallas kernels for 0%

commit v1 on v0

v1 whole, which is shorter than its diff:
```python
import functools
import math

import jax
import jax.numpy as jnp
from jax import lax
from jax.experimental import pallas as pl
from jax.experimental.pallas import tpu as pltpu
from jax.sharding import PartitionSpec as P

HDIM = 128
EXP2_SCALE = math.log2(math.e) / math.sqrt(HDIM)
FETCH_FLOPS = 1_500_000_000
CHAINS = 2
CODE_SPAN = 250.0
VMEM_SPEC = pl.BlockSpec(memory_space=pltpu.VMEM)


def copy_kernel(source_ref, out_ref):
    out_ref[...] = source_ref[...]


def join_kernel(here_ref, there_ref, *out_refs):
    for index, ref in enumerate(out_refs):
        width = ref.shape[1]
        columns = slice(index * width, (index + 1) * width)
        ref[...] = jnp.concatenate([here_ref[:, columns], there_ref[:, columns]], axis=0)


def attend_kernel(
    query_here_ref, query_there_ref, key_ref, value_ref, keep_ref, send_ref, dots_ref, weights_ref, *, first_head
):
    half, width = query_here_ref.shape
    rows = 2 * half
    heads = width // HDIM
    slots = dots_ref.shape[0]

    def shifted(head):
        return slice((first_head + head) * HDIM, (first_head + head + 1) * HDIM)

    def score(head):
        columns = slice(head * HDIM, (head + 1) * HDIM)
        dots_ref[head % slots] = lax.dot_general(
            jnp.concatenate([query_here_ref[:, columns], query_there_ref[:, columns]], axis=0),
            key_ref[:, shifted(head)],
            (((1,), (1,)), ((), ())),
            preferred_element_type=jnp.float32,
        )

    def weigh(head):
        dots = dots_ref[head % slots]
        peak = jnp.max(dots, axis=1, keepdims=True)
        weights = jnp.exp2((dots - peak) * EXP2_SCALE)
        total = jnp.sum(weights, axis=1, keepdims=True)
        coarse = weights.astype(jnp.bfloat16)
        weights_ref[head % slots, :rows] = coarse
        weights_ref[head % slots, rows:] = (weights - coarse.astype(jnp.float32)).astype(jnp.bfloat16)
        for ref, first in ((keep_ref, 0), (send_ref, half)):
            ref[:, width + head : width + head + 1] = peak[first : first + half]
            ref[:, width + HDIM + head : width + HDIM + head + 1] = total[first : first + half]

    def accumulate(head):
        columns = slice(head * HDIM, (head + 1) * HDIM)
        sums = jnp.dot(weights_ref[head % slots], value_ref[:, shifted(head)], preferred_element_type=jnp.float32)
        numerator = sums[:rows] + sums[rows:]
        keep_ref[:, columns] = numerator[:half]
        send_ref[:, columns] = numerator[half:]

    group = slots // 2
    for ref in (keep_ref, send_ref):
        ref[:, width:] = jnp.zeros((half, 2 * HDIM), jnp.float32)
    steps = heads // group
    for step in range(steps + 2):
        for member in range(group):
            for stage, lag in ((score, 0), (weigh, 1), (accumulate, 2)):
                if 0 <= step - lag < steps:
                    stage((step - lag) * group + member)


def pack_exact(values, heads):
    lane = lax.broadcasted_iota(jnp.int32, values.shape, 1)
    first = values.astype(jnp.bfloat16).astype(jnp.float32)
    rest = values - first
    second = rest.astype(jnp.bfloat16).astype(jnp.float32)
    third = rest - second
    tail = jnp.where(lane < 2 * heads, pltpu.roll(second, heads, 1), pltpu.roll(third, 2 * heads, 1))
    return jnp.where(lane < heads, first, tail).astype(jnp.bfloat16)


def unpack_exact(packed, heads):
    terms = packed.astype(jnp.float32)
    return terms + (pltpu.roll(terms, HDIM - heads, 1) + pltpu.roll(terms, HDIM - 2 * heads, 1))


def read_statistics(ref, width, coded):
    if not coded:
        return ref[:, width : width + HDIM], ref[:, width + HDIM :], None
    heads = width // HDIM
    maxima = unpack_exact(ref[:, width : width + HDIM], heads)
    denominators = unpack_exact(ref[:, width + HDIM : width + 2 * HDIM], heads)
    return maxima, denominators, ref[:, width + 2 * HDIM :].astype(jnp.float32) * (1.0 / CODE_SPAN)


def read_numerator(ref, columns, coded):
    if not coded:
        return ref[:, columns]
    code = ref[:, columns].astype(jnp.float32)
    size = jnp.log2(jnp.abs(code)) + CODE_SPAN / 2
    return jnp.where(code < 0, -size, size)


def combine(refs, coded, width):
    statistics = [read_statistics(ref, width, kind == "coded") for ref, kind in zip(refs, coded)]
    maxima = functools.reduce(jnp.maximum, [m for m, _, _ in statistics])
    scales = [jnp.exp2((m - maxima) * EXP2_SCALE) for m, _, _ in statistics]
    denominators = sum(scale * d for scale, (_, d, _) in zip(scales, statistics))
    inverse = 1.0 / denominators
    factors = []
    for kind, scale, (_, d, unit) in zip(coded, scales, statistics):
        factor = scale * inverse
        if kind != "sums":
            factor = factor * d
        factors.append(factor if unit is None else factor * unit)
    return maxima, denominators, factors


def combined_mean(refs, coded, factors, head):
    columns = slice(head * HDIM, (head + 1) * HDIM)
    lane = slice(head, head + 1)
    return sum(f[:, lane] * read_numerator(ref, columns, k == "coded") for ref, k, f in zip(refs, coded, factors))


def section(ref, index, width):
    return ref.at[:, index * width : (index + 1) * width]


def merge_kernel(*refs, kinds, chains):
    all_keep_ref, all_send_ref, means_ref = refs[2 * chains :]
    half, width = means_ref.shape
    heads = width // HDIM
    lane = lax.broadcasted_iota(jnp.int32, (half, HDIM), 1)
    for chain in range(chains):
        sources = refs[2 * chain : 2 * chain + 2]
        keep_ref = section(all_keep_ref, chain, width + 2 * HDIM)
        send_ref = section(all_send_ref, chain, width + 3 * HDIM)
        maxima, denominators, factors = combine(sources, kinds, width)
        largest = jnp.ones((half, HDIM), jnp.float32)
        for head in range(heads):
            columns = slice(head * HDIM, (head + 1) * HDIM)
            merged = combined_mean(sources, kinds, factors, head)
            keep_ref[:, columns] = merged[:half]
            means_ref[:, columns] = merged[half:]
            largest = jnp.where(lane == head, jnp.max(jnp.abs(merged[half:]), axis=1, keepdims=True), largest)
        units = (jnp.maximum(largest, 1e-30) * 1.01).astype(jnp.bfloat16)
        steps = CODE_SPAN / units.astype(jnp.float32)
        for head in range(heads):
            columns = slice(head * HDIM, (head + 1) * HDIM)
            mean = means_ref[:, columns]
            code = jnp.exp2(jnp.abs(mean) * steps[:, head : head + 1] - CODE_SPAN / 2)
            send_ref[:, columns] = jnp.where(mean < 0, -code, code).astype(jnp.bfloat16)
        keep_ref[:, width : width + HDIM] = maxima[:half]
        keep_ref[:, width + HDIM :] = denominators[:half]
        send_ref[:, width : width + HDIM] = pack_exact(maxima[half:], heads)
        send_ref[:, width + HDIM : width + 2 * HDIM] = pack_exact(denominators[half:], heads)
        send_ref[:, width + 2 * HDIM :] = units


def finish_kernel(all_here_ref, all_there_ref, gain_ref, out_ref, *, kinds, chains):
    rows, all_width = out_ref.shape
    width = all_width // chains
    squares = jnp.zeros((rows, HDIM), jnp.float32)
    attended = []
    for chain in range(chains):
        sources = (section(all_here_ref, chain, width + 2 * HDIM), section(all_there_ref, chain, width + 3 * HDIM))
        _, _, factors = combine(sources, kinds, width)
        for head in range(width // HDIM):
            block = combined_mean(sources, kinds, factors, head)
            squares = squares + block * block
            attended.append(block)
    mean = jnp.sum(squares, axis=1, keepdims=True) / all_width
    inverse = 1.0 / jnp.sqrt(mean + 1e-06)
    for head, block in enumerate(attended):
        columns = slice(head * HDIM, (head + 1) * HDIM)
        out_ref[:, columns] = (block * inverse * gain_ref[:, columns]).astype(out_ref.dtype)


def call(kernel, out_shape, operands, flops=0, scratch=(), limit=4 << 20):
    outs = out_shape if isinstance(out_shape, (tuple, list)) else [out_shape]
    size = sum(math.prod(a.shape) * a.dtype.itemsize for a in (*operands, *outs))
    return pl.pallas_call(
        kernel,
        out_shape=out_shape,
        in_specs=[VMEM_SPEC] * len(operands),
        out_specs=jax.tree.map(lambda _: VMEM_SPEC, out_shape),
        scratch_shapes=scratch,
        cost_estimate=pl.CostEstimate(flops=flops, bytes_accessed=size, transcendentals=0),
        compiler_params=pltpu.CompilerParams(vmem_limit_bytes=limit),
    )(*operands)


def exchange(array, mask):
    return lax.ppermute(array, "seq", [(i, i ^ mask) for i in range(lax.axis_size("seq"))])


def shards(queries, keys, values, gain):
    masks = [1 << bit for bit in range(lax.axis_size("seq").bit_length() - 1)]
    core, chips = masks[0], masks[1:]
    rows, width = queries.shape
    part = width // CHAINS
    tokens = keys.shape[0]
    gain = call(copy_kernel, jax.ShapeDtypeStruct((1, width), gain.dtype), [gain.reshape(1, width)], FETCH_FLOPS)

    def joined(window, arrived, parts):
        shape = jax.ShapeDtypeStruct((2 * window.shape[0], window.shape[1] // parts), window.dtype)
        return call(join_kernel, (shape,) * parts, [window, arrived], FETCH_FLOPS)

    windows = joined(queries, exchange(queries, chips[-1]), CHAINS)
    for mask in chips[-2::-1]:
        arrived = [exchange(w, mask) for w in windows]
        windows = [joined(w, a, 1)[0] for w, a in zip(windows, arrived)]
    arrived = [exchange(w, core) for w in windows]
    half = windows[0].shape[0]

    plain = lambda count, parts: jax.ShapeDtypeStruct((count, parts * (part + 2 * HDIM)), jnp.float32)
    code = lambda count, parts: jax.ShapeDtypeStruct((count, parts * (part + 3 * HDIM)), jnp.bfloat16)

    def attend(chain):
        return call(
            functools.partial(attend_kernel, first_head=chain * part // HDIM),
            (plain(half, 1), plain(half, 1)),
            (windows[chain], arrived[chain], keys, values),
            8 * half * tokens * part,
            [pltpu.VMEM((4, 2 * half, tokens), jnp.float32), pltpu.VMEM((4, 4 * half, tokens), jnp.bfloat16)],
            16 << 20,
        )

    def merge(sources, kinds, count, chains):
        kernel = functools.partial(merge_kernel, kinds=kinds, chains=chains)
        shapes = (plain(count, chains), code(count, chains))
        return call(kernel, shapes, sources, 0, [pltpu.VMEM((count, part), jnp.float32)])

    parts = [attend(chain) for chain in range(CHAINS)]
    pairs = [(keep, exchange(send, core)) for keep, send in parts]
    kinds = ("sums", "sums")
    for mask in chips[:-1]:
        half = half // 2
        parts = [merge(pair, kinds, half, 1) for pair in pairs]
        pairs = [(keep, exchange(send, mask)) for keep, send in parts]
        kinds = ("means", "coded")
    keep, send = merge([array for pair in pairs for array in pair], kinds, half // 2, CHAINS)
    kernel = functools.partial(finish_kernel, kinds=("means", "coded"), chains=CHAINS)
    out = jax.ShapeDtypeStruct((rows, width), jnp.bfloat16)
    return call(kernel, out, (keep, exchange(send, chips[-1]), gain), 0)


def solution(mesh):
    spec = P(("grp", "seq"), None)
    return jax.shard_map(shards, mesh=mesh, in_specs=(spec, spec, spec, P()), out_specs=spec, check_vma=False)
```

time: 48.3 us -> 46 us (0.952)
  waiting for transfers between devices: 21.8 us -> 14.5 us
  starting transfers between devices: 13.8 us -> 17.6 us
  Pallas kernels: 11.7 us -> 12.8 us
    ppermute x8 -> x14, waiting for transfers between devices: 21.8 us -> 14.5 us  [exchange(): lax.ppermute(array, 'seq', [(i, i ^ mask) for i in range(lax.axis_size('s...]
    ppermute x8 -> x14, starting transfers between devices: 13.8 us -> 17.6 us  [exchange(): lax.ppermute(array, 'seq', [(i, i ^ mask) for i in range(lax.axis_size('s...]
    pallas_call x9 -> x14, Pallas kernels: 11.7 us -> 12.8 us  [call(): pl.pallas_call(kernel, out_shape=out_shape, in_specs=[VMEM_SPEC] * len(op...]
  transfers between devices with their start and end apart: 8 -> 14, of which waited for: 8 -> 9; matrix products, arithmetic and copies ran while one was open for 0% -> 0% of each run, Pallas kernels for 0% -> 21%
where the time goes in v1:
time: 46 us; the launch traced here: 45.9 us
  starting transfers between devices  17.6 us (38%)
  waiting for transfers between devices  14.5 us (32%)
  Pallas kernels  12.8 us (28%)
  local copies, waits for them, and re-layouts  0.81 us (2%)
    ppermute x14, starting transfers between devices, exchange(): lax.ppermute(array, 'seq', [(i, i ^ mask) for i in range(lax.axis_size('s...  17.6 us
    ppermute x14, waiting for transfers between devices, exchange(): lax.ppermute(array, 'seq', [(i, i ^ mask) for i in range(lax.axis_size('s...  14.5 us
    pallas_call x14, Pallas kernels, call(): pl.pallas_call(kernel, out_shape=out_shape, in_specs=[VMEM_SPEC] * len(op...  12.8 us
  transfers between devices with their start and end apart: 14, of which 9 were waited for; matrix products, arithmetic and copies ran while one was open for 0% of the time, Pallas kernels for 21%

profile of v1, /device:TPU:0, one launch (start us, length us, event | category | flops | bytes accessed | tf_op | source)
XLA Modules:
  0.0 45.9 jit_solution(17127377333220179711)
XLA Ops:
  0.0 4.1 %collective-permute-start = (bf16[4,5120]{1,0:T(4,128)(2,1)}, bf16[4,5120]{1,0:T(4,128)(2,1)S(1)}, u32[]{:S(2)}, u32[]{:S(2)}) collective-permute-start(bf16[4,5120]{1,0:T(4,128)(2,1)} %here_ref.1), channel_id=1, source_target_pairs={{0,8},{1,9},{2,10},{3,11},{4,12},{5,13},{6,14},{7,15},{8,0},{9,1},... | collective-permute-start | bytes 122888 | tf_op jit(solution)/shard_map/ppermute | solution.py:202
  4.1 2.6 %collective-permute-done.there_ref = bf16[4,5120]{1,0:T(4,128)(2,1)S(1)} collective-permute-done((bf16[4,5120]{1,0:T(4,128)(2,1)}, bf16[4,5120]{1,0:T(4,128)(2,1)S(1)}, u32[]{:S(2)}, u32[]{:S(2)}) %collective-permute-start) | collective-permute-done | bytes 40992 | tf_op jit(solution)/shard_map/ppermute | solution.py:202
  7.5 1.5 %collective-permute-start.1 = (bf16[8,2560]{1,0:T(8,128)(2,1)S(1)}, bf16[8,2560]{1,0:T(8,128)(2,1)S(1)}, u32[]{:S(2)}, u32[]{:S(2)}) collective-permute-start(bf16[8,2560]{1,0:T(8,128)(2,1)S(1)} %get-tuple-element.21.here_ref), channel_id=1, source_target_pairs={{0,4},{1,5},{2,6},{3,7},{4,0},{5,1},{6,2},{7,3},{8,12},{9,13},{10,... | collective-permute-start | bytes 122888 | tf_op jit(solution)/shard_map/ppermute | solution.py:202
  9.6 2.0 %collective-permute-done.1.there_ref = bf16[8,2560]{1,0:T(8,128)(2,1)S(1)} collective-permute-done((bf16[8,2560]{1,0:T(8,128)(2,1)S(1)}, bf16[8,2560]{1,0:T(8,128)(2,1)S(1)}, u32[]{:S(2)}, u32[]{:S(2)}) %collective-permute-start.1) | collective-permute-done | bytes 40992 | tf_op jit(solution)/shard_map/ppermute | solution.py:202
  11.6 1.8 %collective-permute-start.2 = (bf16[16,2560]{1,0:T(8,128)(2,1)S(1)}, bf16[16,2560]{1,0:T(8,128)(2,1)S(1)}, u32[]{:S(2)}, u32[]{:S(2)}) collective-permute-start(bf16[16,2560]{1,0:T(8,128)(2,1)S(1)} %shard_map.47.here_ref), channel_id=1, source_target_pairs={{0,2},{1,3},{2,0},{3,1},{4,6},{5,7},{6,4},{7,5},{8,10},{9,11},{10,... | collective-permute-start | bytes 245768 | tf_op jit(solution)/shard_map/ppermute | solution.py:202
  13.4 1.2 %collective-permute-start.8 = (bf16[16,2560]{1,0:T(8,128)(2,1)S(1)}, bf16[16,2560]{1,0:T(8,128)(2,1)S(1)}, u32[]{:S(2)}, u32[]{:S(2)}) collective-permute-start(bf16[16,2560]{1,0:T(8,128)(2,1)S(1)} %shard_map.52.here_ref), channel_id=1, source_target_pairs={{0,2},{1,3},{2,0},{3,1},{4,6},{5,7},{6,4},{7,5},{8,10},{9,11},{10,... | collective-permute-start | bytes 245768 | tf_op jit(solution)/shard_map/ppermute | solution.py:202
  14.7 1.4 %collective-permute-done.2.there_ref = bf16[16,2560]{1,0:T(8,128)(2,1)S(1)} collective-permute-done((bf16[16,2560]{1,0:T(8,128)(2,1)S(1)}, bf16[16,2560]{1,0:T(8,128)(2,1)S(1)}, u32[]{:S(2)}, u32[]{:S(2)}) %collective-permute-start.2) | collective-permute-done | bytes 81952 | tf_op jit(solution)/shard_map/ppermute | solution.py:202
  16.2 1.8 %collective-permute-done.8.there_ref = bf16[16,2560]{1,0:T(8,128)(2,1)S(1)} collective-permute-done((bf16[16,2560]{1,0:T(8,128)(2,1)S(1)}, bf16[16,2560]{1,0:T(8,128)(2,1)S(1)}, u32[]{:S(2)}, u32[]{:S(2)}) %collective-permute-start.8) | collective-permute-done | bytes 81952 | tf_op jit(solution)/shard_map/ppermute | solution.py:202
  18.1 1.9 %shard_map.49 = (f32[32,2816]{1,0:T(8,128)S(1)}, f32[32,2816]{1,0:T(8,128)S(1)}) custom-call(bf16[32,2560]{1,0:T(8,128)(2,1)S(1)} %shard_map.48.query_here_ref, bf16[32,2560]{1,0:T(8,128)(2,1)S(1)} %collective-permute-done.3.query_there_ref, bf16[512,5120]{1,0:T(8,128)(2,1)S(1)} %bitcast.2, bf16[512,5120]{1,0:T(8,128)(2,1)S(1)} %bitcast.4), custom_call_target="tpu_custom_call" | custom-call | flops 335544320 | bytes 11534336 | tf_op jit(solution)/shard_map/pallas_call | solution.py:190
  20.6 1.9 %shard_map.54 = (f32[32,2816]{1,0:T(8,128)S(1)}, f32[32,2816]{1,0:T(8,128)S(1)}) custom-call(bf16[32,2560]{1,0:T(8,128)(2,1)S(1)} %shard_map.53.query_here_ref, bf16[32,2560]{1,0:T(8,128)(2,1)S(1)} %collective-permute-done.9.query_there_ref, bf16[512,5120]{1,0:T(8,128)(2,1)S(1)} %bitcast.2, bf16[512,5120]{1,0:T(8,128)(2,1)S(1)} %bitcast.4), custom_call_target="tpu_custom_call" | custom-call | flops 335544320 | bytes 11534336 | tf_op jit(solution)/shard_map/pallas_call | solution.py:190
  22.7 2.0 %shard_map.50 = (f32[16,2816]{1,0:T(8,128)S(1)}, bf16[16,2944]{1,0:T(8,128)(2,1)S(1)}) custom-call(f32[32,2816]{1,0:T(8,128)S(1)} %get-tuple-element.22.refs_0_, f32[32,2816]{1,0:T(8,128)S(1)} %collective-permute-done.4.refs_1_), custom_call_target="tpu_custom_call" | custom-call | bytes 995328 | tf_op jit(solution)/shard_map/pallas_call | solution.py:190
  24.6 1.3 %collective-permute-start.5 = (bf16[16,2944]{1,0:T(8,128)(2,1)S(1)}, bf16[16,2944]{1,0:T(8,128)(2,1)S(1)}, u32[]{:S(2)}, u32[]{:S(2)}) collective-permute-start(bf16[16,2944]{1,0:T(8,128)(2,1)S(1)} %get-tuple-element.25), channel_id=1, source_target_pairs={{0,2},{1,3},{2,0},{3,1},{4,6},{5,7},{6,4},{7,5},{8,10},{9,11},{10,... | collective-permute-start | bytes 282632 | tf_op jit(solution)/shard_map/ppermute | solution.py:202
  25.9 2.0 %shard_map.55 = (f32[16,2816]{1,0:T(8,128)S(1)}, bf16[16,2944]{1,0:T(8,128)(2,1)S(1)}) custom-call(f32[32,2816]{1,0:T(8,128)S(1)} %get-tuple-element.29.refs_0_, f32[32,2816]{1,0:T(8,128)S(1)} %collective-permute-done.10.refs_1_), custom_call_target="tpu_custom_call" | custom-call | bytes 995328 | tf_op jit(solution)/shard_map/pallas_call | solution.py:190
  27.9 0.9 %collective-permute-start.11 = (bf16[16,2944]{1,0:T(8,128)(2,1)S(1)}, bf16[16,2944]{1,0:T(8,128)(2,1)S(1)}, u32[]{:S(2)}, u32[]{:S(2)}) collective-permute-start(bf16[16,2944]{1,0:T(8,128)(2,1)S(1)} %get-tuple-element.32), channel_id=1, source_target_pairs={{0,2},{1,3},{2,0},{3,1},{4,6},{5,7},{6,4},{7,5},{8,10},{9,11},{10,... | collective-permute-start | bytes 282632 | tf_op jit(solution)/shard_map/ppermute | solution.py:202
  28.8 1.0 %collective-permute-done.5.refs_1_ = bf16[16,2944]{1,0:T(8,128)(2,1)S(1)} collective-permute-done((bf16[16,2944]{1,0:T(8,128)(2,1)S(1)}, bf16[16,2944]{1,0:T(8,128)(2,1)S(1)}, u32[]{:S(2)}, u32[]{:S(2)}) %collective-permute-start.5) | collective-permute-done | bytes 94240 | tf_op jit(solution)/shard_map/ppermute | solution.py:202
  29.8 0.9 %shard_map.51 = (f32[8,2816]{1,0:T(8,128)S(1)}, bf16[8,2944]{1,0:T(8,128)(2,1)S(1)}) custom-call(f32[16,2816]{1,0:T(8,128)S(1)} %get-tuple-element.24.refs_0_, bf16[16,2944]{1,0:T(8,128)(2,1)S(1)} %collective-permute-done.5.refs_1_), custom_call_target="tpu_custom_call" | custom-call | bytes 411648 | tf_op jit(solution)/shard_map/pallas_call | solution.py:190
  30.7 1.3 %collective-permute-start.6 = (bf16[8,2944]{1,0:T(8,128)(2,1)S(1)}, bf16[8,2944]{1,0:T(8,128)(2,1)S(1)}, u32[]{:S(2)}, u32[]{:S(2)}) collective-permute-start(bf16[8,2944]{1,0:T(8,128)(2,1)S(1)} %get-tuple-element.27), channel_id=1, source_target_pairs={{0,4},{1,5},{2,6},{3,7},{4,0},{5,1},{6,2},{7,3},{8,12},{9,13},{10,... | collective-permute-start | bytes 141320 | tf_op jit(solution)/shard_map/ppermute | solution.py:202
  32.7 0.9 %shard_map.56 = (f32[8,2816]{1,0:T(8,128)S(1)}, bf16[8,2944]{1,0:T(8,128)(2,1)S(1)}) custom-call(f32[16,2816]{1,0:T(8,128)S(1)} %get-tuple-element.31.refs_0_, bf16[16,2944]{1,0:T(8,128)(2,1)S(1)} %collective-permute-done.11.refs_1_), custom_call_target="tpu_custom_call" | custom-call | bytes 411648 | tf_op jit(solution)/shard_map/pallas_call | solution.py:190
  33.7 1.2 %collective-permute-start.12 = (bf16[8,2944]{1,0:T(8,128)(2,1)S(1)}, bf16[8,2944]{1,0:T(8,128)(2,1)S(1)}, u32[]{:S(2)}, u32[]{:S(2)}) collective-permute-start(bf16[8,2944]{1,0:T(8,128)(2,1)S(1)} %get-tuple-element.34), channel_id=1, source_target_pairs={{0,4},{1,5},{2,6},{3,7},{4,0},{5,1},{6,2},{7,3},{8,12},{9,13},{10,... | collective-permute-start | bytes 141320 | tf_op jit(solution)/shard_map/ppermute | solution.py:202
  34.9 2.9 %collective-permute-done.12.refs_3_ = bf16[8,2944]{1,0:T(8,128)(2,1)S(1)} collective-permute-done((bf16[8,2944]{1,0:T(8,128)(2,1)S(1)}, bf16[8,2944]{1,0:T(8,128)(2,1)S(1)}, u32[]{:S(2)}, u32[]{:S(2)}) %collective-permute-start.12) | collective-permute-done | bytes 47136 | tf_op jit(solution)/shard_map/ppermute | solution.py:202
  37.8 2.0 %shard_map.57 = (f32[4,5632]{1,0:T(4,128)S(1)}, bf16[4,5888]{1,0:T(4,128)(2,1)S(1)}) custom-call(f32[8,2816]{1,0:T(8,128)S(1)} %get-tuple-element.26.refs_0_, bf16[8,2944]{1,0:T(8,128)(2,1)S(1)} %collective-permute-done.6.refs_1_, f32[8,2816]{1,0:T(8,128)S(1)} %get-tuple-element.33.refs_2_, bf16[8,2944]{1,0:T(8,128)(2,1)S(1)} %collective-permute-done.12.refs_3_), custom_call_target="tpu_custom_call" | custom-call | bytes 411648 | tf_op jit(solution)/shard_map/pallas_call | solution.py:190
  39.8 3.0 %collective-permute-start.13 = (bf16[4,5888]{1,0:T(4,128)(2,1)S(1)}, bf16[4,5888]{1,0:T(4,128)(2,1)S(1)}, u32[]{:S(2)}, u32[]{:S(2)}) collective-permute-start(bf16[4,5888]{1,0:T(4,128)(2,1)S(1)} %get-tuple-element.36), channel_id=1, source_target_pairs={{0,8},{1,9},{2,10},{3,11},{4,12},{5,13},{6,14},{7,15},{8,0},{9,1},... | collective-permute-start | bytes 141320 | tf_op jit(solution)/shard_map/ppermute | solution.py:202
  42.8 2.0 %collective-permute-done.13.all_there_ref = bf16[4,5888]{1,0:T(4,128)(2,1)S(1)} collective-permute-done((bf16[4,5888]{1,0:T(4,128)(2,1)S(1)}, bf16[4,5888]{1,0:T(4,128)(2,1)S(1)}, u32[]{:S(2)}, u32[]{:S(2)}) %collective-permute-start.13) | collective-permute-done | bytes 47136 | tf_op jit(solution)/shard_map/ppermute | solution.py:202
  44.8 1.0 %shard_map.59 = bf16[4,5120]{1,0:T(4,128)(2,1)} custom-call(f32[4,5632]{1,0:T(4,128)S(1)} %get-tuple-element.35.all_here_ref, bf16[4,5888]{1,0:T(4,128)(2,1)S(1)} %collective-permute-done.13.all_there_ref, f32[1,5120]{1,0:T(1,128)S(1)} %shard_map.58.gain_ref), custom_call_target="tpu_custom_call" | custom-call | bytes 198656 | tf_op jit(solution)/shard_map/pallas_call | solution.py:190
  (32 shorter events, 3.0 us)
Async XLA Ops:
  0.0 6.7 %collective-permute-start = (bf16[4,5120]{1,0:T(4,128)(2,1)}, bf16[4,5120]{1,0:T(4,128)(2,1)S(1)}, u32[]{:S(2)}, u32[]{:S(2)}) collective-permute-start(bf16[4,5120]{1,0:T(4,128)(2,1)} %here_ref.1), channel_id=1, source_target_pairs={{0,8},{1,9},{2,10},{3,11},{4,12},{5,13},{6,14},{7,15},{8,0},{9,1},... | collective-permute-start | bytes 122888 | tf_op jit(solution)/shard_map/ppermute | solution.py:202
  6.7 0.8 %copy-start = (bf16[4,5120]{1,0:T(4,128)(2,1)S(1)}, bf16[4,5120]{1,0:T(4,128)(2,1)}, u32[]{:S(2)}) copy-start(bf16[4,5120]{1,0:T(4,128)(2,1)} %here_ref.1) | copy-start | bytes 122884
  7.5 4.1 %collective-permute-start.1 = (bf16[8,2560]{1,0:T(8,128)(2,1)S(1)}, bf16[8,2560]{1,0:T(8,128)(2,1)S(1)}, u32[]{:S(2)}, u32[]{:S(2)}) collective-permute-start(bf16[8,2560]{1,0:T(8,128)(2,1)S(1)} %get-tuple-element.21.here_ref), channel_id=1, source_target_pairs={{0,4},{1,5},{2,6},{3,7},{4,0},{5,1},{6,2},{7,3},{8,12},{9,13},{10,... | collective-permute-start | bytes 122888 | tf_op jit(solution)/shard_map/ppermute | solution.py:202
  9.0 4.3 %collective-permute-start.7 = (bf16[8,2560]{1,0:T(8,128)(2,1)S(1)}, bf16[8,2560]{1,0:T(8,128)(2,1)S(1)}, u32[]{:S(2)}, u32[]{:S(2)}) collective-permute-start(bf16[8,2560]{1,0:T(8,128)(2,1)S(1)} %get-tuple-element.28.here_ref), channel_id=1, source_target_pairs={{0,4},{1,5},{2,6},{3,7},{4,0},{5,1},{6,2},{7,3},{8,12},{9,13},{10,... | collective-permute-start | bytes 122888 | tf_op jit(solution)/shard_map/ppermute | solution.py:202
  11.6 4.5 %collective-permute-start.2 = (bf16[16,2560]{1,0:T(8,128)(2,1)S(1)}, bf16[16,2560]{1,0:T(8,128)(2,1)S(1)}, u32[]{:S(2)}, u32[]{:S(2)}) collective-permute-start(bf16[16,2560]{1,0:T(8,128)(2,1)S(1)} %shard_map.47.here_ref), channel_id=1, source_target_pairs={{0,2},{1,3},{2,0},{3,1},{4,6},{5,7},{6,4},{7,5},{8,10},{9,11},{10,... | collective-permute-start | bytes 245768 | tf_op jit(solution)/shard_map/ppermute | solution.py:202
  13.4 4.7 %slice-start = ((s8[5242880]{0:T(1024)(128)(4,1)}), s8[4194304]{0:T(1024)(128)(4,1)S(1)}, s32[]{:S(2)}) async-start(s8[5242880]{0:T(1024)(128)(4,1)} %bitcast.1), calls=%async_computation | async-start | bytes 8388608
  13.4 4.7 %slice-start.2 = ((s8[5242880]{0:T(1024)(128)(4,1)}), s8[4194304]{0:T(1024)(128)(4,1)S(1)}, s32[]{:S(2)}) async-start(s8[5242880]{0:T(1024)(128)(4,1)} %bitcast.3), calls=%async_computation.2 | async-start | bytes 8388608
  13.4 4.7 %slice-start.1 = ((s8[5242880]{0:T(1024)(128)(4,1)}), s8[1048576]{0:T(1024)(128)(4,1)S(1)}, s32[]{:S(2)}) async-start(s8[5242880]{0:T(1024)(128)(4,1)} %bitcast.1), calls=%async_computation.1 | async-start | bytes 2097152
  13.4 4.7 %slice-start.3 = ((s8[5242880]{0:T(1024)(128)(4,1)}), s8[1048576]{0:T(1024)(128)(4,1)S(1)}, s32[]{:S(2)}) async-start(s8[5242880]{0:T(1024)(128)(4,1)} %bitcast.3), calls=%async_computation.3 | async-start | bytes 2097152
  13.4 4.5 %collective-permute-start.8 = (bf16[16,2560]{1,0:T(8,128)(2,1)S(1)}, bf16[16,2560]{1,0:T(8,128)(2,1)S(1)}, u32[]{:S(2)}, u32[]{:S(2)}) collective-permute-start(bf16[16,2560]{1,0:T(8,128)(2,1)S(1)} %shard_map.52.here_ref), channel_id=1, source_target_pairs={{0,2},{1,3},{2,0},{3,1},{4,6},{5,7},{6,4},{7,5},{8,10},{9,11},{10,... | collective-permute-start | bytes 245768 | tf_op jit(solution)/shard_map/ppermute | solution.py:202
  16.1 1.9 %collective-permute-start.3 = (bf16[32,2560]{1,0:T(8,128)(2,1)S(1)}, bf16[32,2560]{1,0:T(8,128)(2,1)S(1)}, u32[]{:S(2)}, u32[]{:S(2)}) collective-permute-start(bf16[32,2560]{1,0:T(8,128)(2,1)S(1)} %shard_map.48.query_here_ref), channel_id=1, source_target_pairs={{0,1},{1,0},{2,3},{3,2},{4,5},{5,4},{6,7},{7,6},{8,9},{9,8},{10,11... | collective-permute-start | bytes 491528 | tf_op jit(solution)/shard_map/ppermute | solution.py:202
  18.0 2.7 %collective-permute-start.9 = (bf16[32,2560]{1,0:T(8,128)(2,1)S(1)}, bf16[32,2560]{1,0:T(8,128)(2,1)S(1)}, u32[]{:S(2)}, u32[]{:S(2)}) collective-permute-start(bf16[32,2560]{1,0:T(8,128)(2,1)S(1)} %shard_map.53.query_here_ref), channel_id=1, source_target_pairs={{0,1},{1,0},{2,3},{3,2},{4,5},{5,4},{6,7},{7,6},{8,9},{9,8},{10,11... | collective-permute-start | bytes 491528 | tf_op jit(solution)/shard_map/ppermute | solution.py:202
  20.1 22.7 %copy-start.1 = (f32[5120]{0:T(1024)S(1)}, f32[5120]{0:T(1024)}, u32[]{:S(2)}) copy-start(f32[5120]{0:T(1024)} %param.7) | copy-start | bytes 61444
  20.1 2.6 %collective-permute-start.4 = (f32[32,2816]{1,0:T(8,128)S(1)}, f32[32,2816]{1,0:T(8,128)S(1)}, u32[]{:S(2)}, u32[]{:S(2)}) collective-permute-start(f32[32,2816]{1,0:T(8,128)S(1)} %get-tuple-element.23), channel_id=1, source_target_pairs={{0,1},{1,0},{2,3},{3,2},{4,5},{5,4},{6,7},{7,6},{8,9},{9,8},{10,11... | collective-permute-start | bytes 1081352 | tf_op jit(solution)/shard_map/ppermute | solution.py:202
  22.6 3.4 %collective-permute-start.10 = (f32[32,2816]{1,0:T(8,128)S(1)}, f32[32,2816]{1,0:T(8,128)S(1)}, u32[]{:S(2)}, u32[]{:S(2)}) collective-permute-start(f32[32,2816]{1,0:T(8,128)S(1)} %get-tuple-element.30), channel_id=1, source_target_pairs={{0,1},{1,0},{2,3},{3,2},{4,5},{5,4},{6,7},{7,6},{8,9},{9,8},{10,11... | collective-permute-start | bytes 1081352 | tf_op jit(solution)/shard_map/ppermute | solution.py:202
  24.6 5.2 %collective-permute-start.5 = (bf16[16,2944]{1,0:T(8,128)(2,1)S(1)}, bf16[16,2944]{1,0:T(8,128)(2,1)S(1)}, u32[]{:S(2)}, u32[]{:S(2)}) collective-permute-start(bf16[16,2944]{1,0:T(8,128)(2,1)S(1)} %get-tuple-element.25), channel_id=1, source_target_pairs={{0,2},{1,3},{2,0},{3,1},{4,6},{5,7},{6,4},{7,5},{8,10},{9,11},{10,... | collective-permute-start | bytes 282632 | tf_op jit(solution)/shard_map/ppermute | solution.py:202
  27.9 4.8 %collective-permute-start.11 = (bf16[16,2944]{1,0:T(8,128)(2,1)S(1)}, bf16[16,2944]{1,0:T(8,128)(2,1)S(1)}, u32[]{:S(2)}, u32[]{:S(2)}) collective-permute-start(bf16[16,2944]{1,0:T(8,128)(2,1)S(1)} %get-tuple-element.32), channel_id=1, source_target_pairs={{0,2},{1,3},{2,0},{3,1},{4,6},{5,7},{6,4},{7,5},{8,10},{9,11},{10,... | collective-permute-start | bytes 282632 | tf_op jit(solution)/shard_map/ppermute | solution.py:202
  30.7 4.1 %collective-permute-start.6 = (bf16[8,2944]{1,0:T(8,128)(2,1)S(1)}, bf16[8,2944]{1,0:T(8,128)(2,1)S(1)}, u32[]{:S(2)}, u32[]{:S(2)}) collective-permute-start(bf16[8,2944]{1,0:T(8,128)(2,1)S(1)} %get-tuple-element.27), channel_id=1, source_target_pairs={{0,4},{1,5},{2,6},{3,7},{4,0},{5,1},{6,2},{7,3},{8,12},{9,13},{10,... | collective-permute-start | bytes 141320 | tf_op jit(solution)/shard_map/ppermute | solution.py:202
  33.7 4.1 %collective-permute-start.12 = (bf16[8,2944]{1,0:T(8,128)(2,1)S(1)}, bf16[8,2944]{1,0:T(8,128)(2,1)S(1)}, u32[]{:S(2)}, u32[]{:S(2)}) collective-permute-start(bf16[8,2944]{1,0:T(8,128)(2,1)S(1)} %get-tuple-element.34), channel_id=1, source_target_pairs={{0,4},{1,5},{2,6},{3,7},{4,0},{5,1},{6,2},{7,3},{8,12},{9,13},{10,... | collective-permute-start | bytes 141320 | tf_op jit(solution)/shard_map/ppermute | solution.py:202
  39.8 5.0 %collective-permute-start.13 = (bf16[4,5888]{1,0:T(4,128)(2,1)S(1)}, bf16[4,5888]{1,0:T(4,128)(2,1)S(1)}, u32[]{:S(2)}, u32[]{:S(2)}) collective-permute-start(bf16[4,5888]{1,0:T(4,128)(2,1)S(1)} %get-tuple-element.36), channel_id=1, source_target_pairs={{0,8},{1,9},{2,10},{3,11},{4,12},{5,13},{6,14},{7,15},{8,0},{9,1},... | collective-permute-start | bytes 141320 | tf_op jit(solution)/shard_map/ppermute | solution.py:202

commit v2 on v1

--- a/solution.py
+++ b/solution.py
@@ -144,25 +144,25 @@
         keep_ref = section(all_keep_ref, chain, width + 2 * HDIM)
         send_ref = section(all_send_ref, chain, width + 3 * HDIM)
         maxima, denominators, factors = combine(sources, kinds, width)
-        largest = jnp.ones((half, HDIM), jnp.float32)
+        largest = jnp.full((half, HDIM), 1e-30, jnp.float32)
         for head in range(heads):
             columns = slice(head * HDIM, (head + 1) * HDIM)
             merged = combined_mean(sources, kinds, factors, head)
             keep_ref[:, columns] = merged[:half]
             means_ref[:, columns] = merged[half:]
-            largest = jnp.where(lane == head, jnp.max(jnp.abs(merged[half:]), axis=1, keepdims=True), largest)
-        units = (jnp.maximum(largest, 1e-30) * 1.01).astype(jnp.bfloat16)
-        steps = CODE_SPAN / units.astype(jnp.float32)
+            largest = jnp.maximum(largest, jnp.abs(merged[half:]))
+        units = (jnp.max(largest, axis=1, keepdims=True) * 1.01).astype(jnp.bfloat16)
+        step = jnp.broadcast_to(CODE_SPAN / units.astype(jnp.float32), largest.shape)
         for head in range(heads):
             columns = slice(head * HDIM, (head + 1) * HDIM)
             mean = means_ref[:, columns]
-            code = jnp.exp2(jnp.abs(mean) * steps[:, head : head + 1] - CODE_SPAN / 2)
+            code = jnp.exp2(jnp.abs(mean) * step - CODE_SPAN / 2)
             send_ref[:, columns] = jnp.where(mean < 0, -code, code).astype(jnp.bfloat16)
         keep_ref[:, width : width + HDIM] = maxima[:half]
         keep_ref[:, width + HDIM :] = denominators[:half]
         send_ref[:, width : width + HDIM] = pack_exact(maxima[half:], heads)
         send_ref[:, width + HDIM : width + 2 * HDIM] = pack_exact(denominators[half:], heads)
-        send_ref[:, width + 2 * HDIM :] = units
+        send_ref[:, width + 2 * HDIM :] = jnp.broadcast_to(units, largest.shape)
 
 
 def finish_kernel(all_here_ref, all_there_ref, gain_ref, out_ref, *, kinds, chains):

time: 46 us -> 41.6 us (0.904)
  Pallas kernels: 12.8 us -> 6.94 us
  waiting for transfers between devices: 14.5 us -> 15.6 us
    pallas_call x14, Pallas kernels: 12.8 us -> 6.94 us  [call(): pl.pallas_call(kernel, out_shape=out_shape, in_specs=[VMEM_SPEC] * len(op...]
    ppermute x14, waiting for transfers between devices: 14.5 us -> 15.6 us  [exchange(): lax.ppermute(array, 'seq', [(i, i ^ mask) for i in range(lax.axis_size('s...]
  transfers between devices with their start and end apart: 14 -> 14, of which waited for: 9 -> 8; matrix products, arithmetic and copies ran while one was open for 0% -> 0% of each run, Pallas kernels for 21% -> 13%
where the time goes in v2:
time: 41.6 us; the launch traced here: 41.4 us
  starting transfers between devices  17.9 us (43%)
  waiting for transfers between devices  15.6 us (38%)
  Pallas kernels  6.94 us (17%)
  local copies, waits for them, and re-layouts  0.81 us (2%)
    ppermute x14, starting transfers between devices, exchange(): lax.ppermute(array, 'seq', [(i, i ^ mask) for i in range(lax.axis_size('s...  17.9 us
    ppermute x14, waiting for transfers between devices, exchange(): lax.ppermute(array, 'seq', [(i, i ^ mask) for i in range(lax.axis_size('s...  15.6 us
    pallas_call x14, Pallas kernels, call(): pl.pallas_call(kernel, out_shape=out_shape, in_specs=[VMEM_SPEC] * len(op...  6.94 us
  transfers between devices with their start and end apart: 14, of which 8 were waited for; matrix products, arithmetic and copies ran while one was open for 0% of the time, Pallas kernels for 13%

profile of v2, /device:TPU:0, one launch (start us, length us, event | category | flops | bytes accessed | tf_op | source)
XLA Modules:
  0.0 41.4 jit_solution(3066164380628287207)
XLA Ops:
  0.0 4.1 %collective-permute-start = (bf16[4,5120]{1,0:T(4,128)(2,1)}, bf16[4,5120]{1,0:T(4,128)(2,1)S(1)}, u32[]{:S(2)}, u32[]{:S(2)}) collective-permute-start(bf16[4,5120]{1,0:T(4,128)(2,1)} %here_ref.1), channel_id=1, source_target_pairs={{0,8},{1,9},{2,10},{3,11},{4,12},{5,13},{6,14},{7,15},{8,0},{9,1},... | collective-permute-start | bytes 122888 | tf_op jit(solution)/shard_map/ppermute | solution.py:202
  4.1 2.6 %collective-permute-done.there_ref = bf16[4,5120]{1,0:T(4,128)(2,1)S(1)} collective-permute-done((bf16[4,5120]{1,0:T(4,128)(2,1)}, bf16[4,5120]{1,0:T(4,128)(2,1)S(1)}, u32[]{:S(2)}, u32[]{:S(2)}) %collective-permute-start) | collective-permute-done | bytes 40992 | tf_op jit(solution)/shard_map/ppermute | solution.py:202
  6.7 0.8 %copy-done = bf16[4,5120]{1,0:T(4,128)(2,1)S(1)} copy-done((bf16[4,5120]{1,0:T(4,128)(2,1)S(1)}, bf16[4,5120]{1,0:T(4,128)(2,1)}, u32[]{:S(2)}) %copy-start) | copy-done | bytes 40984
  7.5 1.5 %collective-permute-start.1 = (bf16[8,2560]{1,0:T(8,128)(2,1)S(1)}, bf16[8,2560]{1,0:T(8,128)(2,1)S(1)}, u32[]{:S(2)}, u32[]{:S(2)}) collective-permute-start(bf16[8,2560]{1,0:T(8,128)(2,1)S(1)} %get-tuple-element.21.here_ref), channel_id=1, source_target_pairs={{0,4},{1,5},{2,6},{3,7},{4,0},{5,1},{6,2},{7,3},{8,12},{9,13},{10,... | collective-permute-start | bytes 122888 | tf_op jit(solution)/shard_map/ppermute | solution.py:202
  9.0 0.6 %collective-permute-start.7 = (bf16[8,2560]{1,0:T(8,128)(2,1)S(1)}, bf16[8,2560]{1,0:T(8,128)(2,1)S(1)}, u32[]{:S(2)}, u32[]{:S(2)}) collective-permute-start(bf16[8,2560]{1,0:T(8,128)(2,1)S(1)} %get-tuple-element.28.here_ref), channel_id=1, source_target_pairs={{0,4},{1,5},{2,6},{3,7},{4,0},{5,1},{6,2},{7,3},{8,12},{9,13},{10,... | collective-permute-start | bytes 122888 | tf_op jit(solution)/shard_map/ppermute | solution.py:202
  9.6 2.0 %collective-permute-done.1.there_ref = bf16[8,2560]{1,0:T(8,128)(2,1)S(1)} collective-permute-done((bf16[8,2560]{1,0:T(8,128)(2,1)S(1)}, bf16[8,2560]{1,0:T(8,128)(2,1)S(1)}, u32[]{:S(2)}, u32[]{:S(2)}) %collective-permute-start.1) | collective-permute-done | bytes 40992 | tf_op jit(solution)/shard_map/ppermute | solution.py:202
  11.6 1.8 %collective-permute-start.2 = (bf16[16,2560]{1,0:T(8,128)(2,1)S(1)}, bf16[16,2560]{1,0:T(8,128)(2,1)S(1)}, u32[]{:S(2)}, u32[]{:S(2)}) collective-permute-start(bf16[16,2560]{1,0:T(8,128)(2,1)S(1)} %shard_map.47.here_ref), channel_id=1, source_target_pairs={{0,2},{1,3},{2,0},{3,1},{4,6},{5,7},{6,4},{7,5},{8,10},{9,11},{10,... | collective-permute-start | bytes 245768 | tf_op jit(solution)/shard_map/ppermute | solution.py:202
  13.4 1.2 %collective-permute-start.8 = (bf16[16,2560]{1,0:T(8,128)(2,1)S(1)}, bf16[16,2560]{1,0:T(8,128)(2,1)S(1)}, u32[]{:S(2)}, u32[]{:S(2)}) collective-permute-start(bf16[16,2560]{1,0:T(8,128)(2,1)S(1)} %shard_map.52.here_ref), channel_id=1, source_target_pairs={{0,2},{1,3},{2,0},{3,1},{4,6},{5,7},{6,4},{7,5},{8,10},{9,11},{10,... | collective-permute-start | bytes 245768 | tf_op jit(solution)/shard_map/ppermute | solution.py:202
  14.7 1.4 %collective-permute-done.2.there_ref = bf16[16,2560]{1,0:T(8,128)(2,1)S(1)} collective-permute-done((bf16[16,2560]{1,0:T(8,128)(2,1)S(1)}, bf16[16,2560]{1,0:T(8,128)(2,1)S(1)}, u32[]{:S(2)}, u32[]{:S(2)}) %collective-permute-start.2) | collective-permute-done | bytes 81952 | tf_op jit(solution)/shard_map/ppermute | solution.py:202
  16.2 1.8 %collective-permute-done.8.there_ref = bf16[16,2560]{1,0:T(8,128)(2,1)S(1)} collective-permute-done((bf16[16,2560]{1,0:T(8,128)(2,1)S(1)}, bf16[16,2560]{1,0:T(8,128)(2,1)S(1)}, u32[]{:S(2)}, u32[]{:S(2)}) %collective-permute-start.8) | collective-permute-done | bytes 81952 | tf_op jit(solution)/shard_map/ppermute | solution.py:202
  18.1 1.9 %shard_map.49 = (f32[32,2816]{1,0:T(8,128)S(1)}, f32[32,2816]{1,0:T(8,128)S(1)}) custom-call(bf16[32,2560]{1,0:T(8,128)(2,1)S(1)} %shard_map.48.query_here_ref, bf16[32,2560]{1,0:T(8,128)(2,1)S(1)} %collective-permute-done.3.query_there_ref, bf16[512,5120]{1,0:T(8,128)(2,1)S(1)} %bitcast.2, bf16[512,5120]{1,0:T(8,128)(2,1)S(1)} %bitcast.4), custom_call_target="tpu_custom_call" | custom-call | flops 335544320 | bytes 11534336 | tf_op jit(solution)/shard_map/pallas_call | solution.py:190
  20.1 0.5 %collective-permute-start.4 = (f32[32,2816]{1,0:T(8,128)S(1)}, f32[32,2816]{1,0:T(8,128)S(1)}, u32[]{:S(2)}, u32[]{:S(2)}) collective-permute-start(f32[32,2816]{1,0:T(8,128)S(1)} %get-tuple-element.23), channel_id=1, source_target_pairs={{0,1},{1,0},{2,3},{3,2},{4,5},{5,4},{6,7},{7,6},{8,9},{9,8},{10,11... | collective-permute-start | bytes 1081352 | tf_op jit(solution)/shard_map/ppermute | solution.py:202
  20.6 1.9 %shard_map.54 = (f32[32,2816]{1,0:T(8,128)S(1)}, f32[32,2816]{1,0:T(8,128)S(1)}) custom-call(bf16[32,2560]{1,0:T(8,128)(2,1)S(1)} %shard_map.53.query_here_ref, bf16[32,2560]{1,0:T(8,128)(2,1)S(1)} %collective-permute-done.9.query_there_ref, bf16[512,5120]{1,0:T(8,128)(2,1)S(1)} %bitcast.2, bf16[512,5120]{1,0:T(8,128)(2,1)S(1)} %bitcast.4), custom_call_target="tpu_custom_call" | custom-call | flops 335544320 | bytes 11534336 | tf_op jit(solution)/shard_map/pallas_call | solution.py:190
  23.1 1.3 %collective-permute-start.5 = (bf16[16,2944]{1,0:T(8,128)(2,1)S(1)}, bf16[16,2944]{1,0:T(8,128)(2,1)S(1)}, u32[]{:S(2)}, u32[]{:S(2)}) collective-permute-start(bf16[16,2944]{1,0:T(8,128)(2,1)S(1)} %get-tuple-element.25), channel_id=1, source_target_pairs={{0,2},{1,3},{2,0},{3,1},{4,6},{5,7},{6,4},{7,5},{8,10},{9,11},{10,... | collective-permute-start | bytes 282632 | tf_op jit(solution)/shard_map/ppermute | solution.py:202
  24.8 1.2 %collective-permute-start.11 = (bf16[16,2944]{1,0:T(8,128)(2,1)S(1)}, bf16[16,2944]{1,0:T(8,128)(2,1)S(1)}, u32[]{:S(2)}, u32[]{:S(2)}) collective-permute-start(bf16[16,2944]{1,0:T(8,128)(2,1)S(1)} %get-tuple-element.32), channel_id=1, source_target_pairs={{0,2},{1,3},{2,0},{3,1},{4,6},{5,7},{6,4},{7,5},{8,10},{9,11},{10,... | collective-permute-start | bytes 282632 | tf_op jit(solution)/shard_map/ppermute | solution.py:202
  26.0 2.8 %collective-permute-done.5.refs_1_ = bf16[16,2944]{1,0:T(8,128)(2,1)S(1)} collective-permute-done((bf16[16,2944]{1,0:T(8,128)(2,1)S(1)}, bf16[16,2944]{1,0:T(8,128)(2,1)S(1)}, u32[]{:S(2)}, u32[]{:S(2)}) %collective-permute-start.5) | collective-permute-done | bytes 94240 | tf_op jit(solution)/shard_map/ppermute | solution.py:202
  29.1 1.3 %collective-permute-start.6 = (bf16[8,2944]{1,0:T(8,128)(2,1)S(1)}, bf16[8,2944]{1,0:T(8,128)(2,1)S(1)}, u32[]{:S(2)}, u32[]{:S(2)}) collective-permute-start(bf16[8,2944]{1,0:T(8,128)(2,1)S(1)} %get-tuple-element.27), channel_id=1, source_target_pairs={{0,4},{1,5},{2,6},{3,7},{4,0},{5,1},{6,2},{7,3},{8,12},{9,13},{10,... | collective-permute-start | bytes 141320 | tf_op jit(solution)/shard_map/ppermute | solution.py:202
  30.8 1.1 %collective-permute-start.12 = (bf16[8,2944]{1,0:T(8,128)(2,1)S(1)}, bf16[8,2944]{1,0:T(8,128)(2,1)S(1)}, u32[]{:S(2)}, u32[]{:S(2)}) collective-permute-start(bf16[8,2944]{1,0:T(8,128)(2,1)S(1)} %get-tuple-element.34), channel_id=1, source_target_pairs={{0,4},{1,5},{2,6},{3,7},{4,0},{5,1},{6,2},{7,3},{8,12},{9,13},{10,... | collective-permute-start | bytes 141320 | tf_op jit(solution)/shard_map/ppermute | solution.py:202
  32.0 1.6 %collective-permute-done.6.refs_1_ = bf16[8,2944]{1,0:T(8,128)(2,1)S(1)} collective-permute-done((bf16[8,2944]{1,0:T(8,128)(2,1)S(1)}, bf16[8,2944]{1,0:T(8,128)(2,1)S(1)}, u32[]{:S(2)}, u32[]{:S(2)}) %collective-permute-start.6) | collective-permute-done | bytes 47136 | tf_op jit(solution)/shard_map/ppermute | solution.py:202
  33.5 1.4 %collective-permute-done.12.refs_3_ = bf16[8,2944]{1,0:T(8,128)(2,1)S(1)} collective-permute-done((bf16[8,2944]{1,0:T(8,128)(2,1)S(1)}, bf16[8,2944]{1,0:T(8,128)(2,1)S(1)}, u32[]{:S(2)}, u32[]{:S(2)}) %collective-permute-start.12) | collective-permute-done | bytes 47136 | tf_op jit(solution)/shard_map/ppermute | solution.py:202
  34.9 0.4 shard_map.57
  35.3 3.0 %collective-permute-start.13 = (bf16[4,5888]{1,0:T(4,128)(2,1)S(1)}, bf16[4,5888]{1,0:T(4,128)(2,1)S(1)}, u32[]{:S(2)}, u32[]{:S(2)}) collective-permute-start(bf16[4,5888]{1,0:T(4,128)(2,1)S(1)} %get-tuple-element.36), channel_id=1, source_target_pairs={{0,8},{1,9},{2,10},{3,11},{4,12},{5,13},{6,14},{7,15},{8,0},{9,1},... | collective-permute-start | bytes 141320 | tf_op jit(solution)/shard_map/ppermute | solution.py:202
  38.3 2.0 %collective-permute-done.13.all_there_ref = bf16[4,5888]{1,0:T(4,128)(2,1)S(1)} collective-permute-done((bf16[4,5888]{1,0:T(4,128)(2,1)S(1)}, bf16[4,5888]{1,0:T(4,128)(2,1)S(1)}, u32[]{:S(2)}, u32[]{:S(2)}) %collective-permute-start.13) | collective-permute-done | bytes 47136 | tf_op jit(solution)/shard_map/ppermute | solution.py:202
  40.4 1.0 %shard_map.59 = bf16[4,5120]{1,0:T(4,128)(2,1)} custom-call(f32[4,5632]{1,0:T(4,128)S(1)} %get-tuple-element.35.all_here_ref, bf16[4,5888]{1,0:T(4,128)(2,1)S(1)} %collective-permute-done.13.all_there_ref, f32[1,5120]{1,0:T(1,128)S(1)} %shard_map.58.gain_ref), custom_call_target="tpu_custom_call" | custom-call | bytes 198656 | tf_op jit(solution)/shard_map/pallas_call | solution.py:190
  (32 shorter events, 1.9 us)
Async XLA Ops:
  0.0 6.7 %collective-permute-start = (bf16[4,5120]{1,0:T(4,128)(2,1)}, bf16[4,5120]{1,0:T(4,128)(2,1)S(1)}, u32[]{:S(2)}, u32[]{:S(2)}) collective-permute-start(bf16[4,5120]{1,0:T(4,128)(2,1)} %here_ref.1), channel_id=1, source_target_pairs={{0,8},{1,9},{2,10},{3,11},{4,12},{5,13},{6,14},{7,15},{8,0},{9,1},... | collective-permute-start | bytes 122888 | tf_op jit(solution)/shard_map/ppermute | solution.py:202
  6.7 0.8 %copy-start = (bf16[4,5120]{1,0:T(4,128)(2,1)S(1)}, bf16[4,5120]{1,0:T(4,128)(2,1)}, u32[]{:S(2)}) copy-start(bf16[4,5120]{1,0:T(4,128)(2,1)} %here_ref.1) | copy-start | bytes 122884
  7.5 4.1 %collective-permute-start.1 = (bf16[8,2560]{1,0:T(8,128)(2,1)S(1)}, bf16[8,2560]{1,0:T(8,128)(2,1)S(1)}, u32[]{:S(2)}, u32[]{:S(2)}) collective-permute-start(bf16[8,2560]{1,0:T(8,128)(2,1)S(1)} %get-tuple-element.21.here_ref), channel_id=1, source_target_pairs={{0,4},{1,5},{2,6},{3,7},{4,0},{5,1},{6,2},{7,3},{8,12},{9,13},{10,... | collective-permute-start | bytes 122888 | tf_op jit(solution)/shard_map/ppermute | solution.py:202
  9.0 4.3 %collective-permute-start.7 = (bf16[8,2560]{1,0:T(8,128)(2,1)S(1)}, bf16[8,2560]{1,0:T(8,128)(2,1)S(1)}, u32[]{:S(2)}, u32[]{:S(2)}) collective-permute-start(bf16[8,2560]{1,0:T(8,128)(2,1)S(1)} %get-tuple-element.28.here_ref), channel_id=1, source_target_pairs={{0,4},{1,5},{2,6},{3,7},{4,0},{5,1},{6,2},{7,3},{8,12},{9,13},{10,... | collective-permute-start | bytes 122888 | tf_op jit(solution)/shard_map/ppermute | solution.py:202
  11.6 4.5 %collective-permute-start.2 = (bf16[16,2560]{1,0:T(8,128)(2,1)S(1)}, bf16[16,2560]{1,0:T(8,128)(2,1)S(1)}, u32[]{:S(2)}, u32[]{:S(2)}) collective-permute-start(bf16[16,2560]{1,0:T(8,128)(2,1)S(1)} %shard_map.47.here_ref), channel_id=1, source_target_pairs={{0,2},{1,3},{2,0},{3,1},{4,6},{5,7},{6,4},{7,5},{8,10},{9,11},{10,... | collective-permute-start | bytes 245768 | tf_op jit(solution)/shard_map/ppermute | solution.py:202
  13.4 4.7 %slice-start = ((s8[5242880]{0:T(1024)(128)(4,1)}), s8[4194304]{0:T(1024)(128)(4,1)S(1)}, s32[]{:S(2)}) async-start(s8[5242880]{0:T(1024)(128)(4,1)} %bitcast.1), calls=%async_computation | async-start | bytes 8388608
  13.4 4.7 %slice-start.2 = ((s8[5242880]{0:T(1024)(128)(4,1)}), s8[4194304]{0:T(1024)(128)(4,1)S(1)}, s32[]{:S(2)}) async-start(s8[5242880]{0:T(1024)(128)(4,1)} %bitcast.3), calls=%async_computation.2 | async-start | bytes 8388608
  13.4 4.7 %slice-start.1 = ((s8[5242880]{0:T(1024)(128)(4,1)}), s8[1048576]{0:T(1024)(128)(4,1)S(1)}, s32[]{:S(2)}) async-start(s8[5242880]{0:T(1024)(128)(4,1)} %bitcast.1), calls=%async_computation.1 | async-start | bytes 2097152
  13.4 4.7 %slice-start.3 = ((s8[5242880]{0:T(1024)(128)(4,1)}), s8[1048576]{0:T(1024)(128)(4,1)S(1)}, s32[]{:S(2)}) async-start(s8[5242880]{0:T(1024)(128)(4,1)} %bitcast.3), calls=%async_computation.3 | async-start | bytes 2097152
  13.4 4.5 %collective-permute-start.8 = (bf16[16,2560]{1,0:T(8,128)(2,1)S(1)}, bf16[16,2560]{1,0:T(8,128)(2,1)S(1)}, u32[]{:S(2)}, u32[]{:S(2)}) collective-permute-start(bf16[16,2560]{1,0:T(8,128)(2,1)S(1)} %shard_map.52.here_ref), channel_id=1, source_target_pairs={{0,2},{1,3},{2,0},{3,1},{4,6},{5,7},{6,4},{7,5},{8,10},{9,11},{10,... | collective-permute-start | bytes 245768 | tf_op jit(solution)/shard_map/ppermute | solution.py:202
  16.1 1.9 %collective-permute-start.3 = (bf16[32,2560]{1,0:T(8,128)(2,1)S(1)}, bf16[32,2560]{1,0:T(8,128)(2,1)S(1)}, u32[]{:S(2)}, u32[]{:S(2)}) collective-permute-start(bf16[32,2560]{1,0:T(8,128)(2,1)S(1)} %shard_map.48.query_here_ref), channel_id=1, source_target_pairs={{0,1},{1,0},{2,3},{3,2},{4,5},{5,4},{6,7},{7,6},{8,9},{9,8},{10,11... | collective-permute-start | bytes 491528 | tf_op jit(solution)/shard_map/ppermute | solution.py:202
  18.0 2.7 %collective-permute-start.9 = (bf16[32,2560]{1,0:T(8,128)(2,1)S(1)}, bf16[32,2560]{1,0:T(8,128)(2,1)S(1)}, u32[]{:S(2)}, u32[]{:S(2)}) collective-permute-start(bf16[32,2560]{1,0:T(8,128)(2,1)S(1)} %shard_map.53.query_here_ref), channel_id=1, source_target_pairs={{0,1},{1,0},{2,3},{3,2},{4,5},{5,4},{6,7},{7,6},{8,9},{9,8},{10,11... | collective-permute-start | bytes 491528 | tf_op jit(solution)/shard_map/ppermute | solution.py:202
  20.1 18.3 %copy-start.1 = (f32[5120]{0:T(1024)S(1)}, f32[5120]{0:T(1024)}, u32[]{:S(2)}) copy-start(f32[5120]{0:T(1024)} %param.7) | copy-start | bytes 61444
  20.1 2.6 %collective-permute-start.4 = (f32[32,2816]{1,0:T(8,128)S(1)}, f32[32,2816]{1,0:T(8,128)S(1)}, u32[]{:S(2)}, u32[]{:S(2)}) collective-permute-start(f32[32,2816]{1,0:T(8,128)S(1)} %get-tuple-element.23), channel_id=1, source_target_pairs={{0,1},{1,0},{2,3},{3,2},{4,5},{5,4},{6,7},{7,6},{8,9},{9,8},{10,11... | collective-permute-start | bytes 1081352 | tf_op jit(solution)/shard_map/ppermute | solution.py:202
  22.6 1.8 %collective-permute-start.10 = (f32[32,2816]{1,0:T(8,128)S(1)}, f32[32,2816]{1,0:T(8,128)S(1)}, u32[]{:S(2)}, u32[]{:S(2)}) collective-permute-start(f32[32,2816]{1,0:T(8,128)S(1)} %get-tuple-element.30), channel_id=1, source_target_pairs={{0,1},{1,0},{2,3},{3,2},{4,5},{5,4},{6,7},{7,6},{8,9},{9,8},{10,11... | collective-permute-start | bytes 1081352 | tf_op jit(solution)/shard_map/ppermute | solution.py:202
  23.1 5.6 %collective-permute-start.5 = (bf16[16,2944]{1,0:T(8,128)(2,1)S(1)}, bf16[16,2944]{1,0:T(8,128)(2,1)S(1)}, u32[]{:S(2)}, u32[]{:S(2)}) collective-permute-start(bf16[16,2944]{1,0:T(8,128)(2,1)S(1)} %get-tuple-element.25), channel_id=1, source_target_pairs={{0,2},{1,3},{2,0},{3,1},{4,6},{5,7},{6,4},{7,5},{8,10},{9,11},{10,... | collective-permute-start | bytes 282632 | tf_op jit(solution)/shard_map/ppermute | solution.py:202
  24.8 5.6 %collective-permute-start.11 = (bf16[16,2944]{1,0:T(8,128)(2,1)S(1)}, bf16[16,2944]{1,0:T(8,128)(2,1)S(1)}, u32[]{:S(2)}, u32[]{:S(2)}) collective-permute-start(bf16[16,2944]{1,0:T(8,128)(2,1)S(1)} %get-tuple-element.32), channel_id=1, source_target_pairs={{0,2},{1,3},{2,0},{3,1},{4,6},{5,7},{6,4},{7,5},{8,10},{9,11},{10,... | collective-permute-start | bytes 282632 | tf_op jit(solution)/shard_map/ppermute | solution.py:202
  29.1 4.5 %collective-permute-start.6 = (bf16[8,2944]{1,0:T(8,128)(2,1)S(1)}, bf16[8,2944]{1,0:T(8,128)(2,1)S(1)}, u32[]{:S(2)}, u32[]{:S(2)}) collective-permute-start(bf16[8,2944]{1,0:T(8,128)(2,1)S(1)} %get-tuple-element.27), channel_id=1, source_target_pairs={{0,4},{1,5},{2,6},{3,7},{4,0},{5,1},{6,2},{7,3},{8,12},{9,13},{10,... | collective-permute-start | bytes 141320 | tf_op jit(solution)/shard_map/ppermute | solution.py:202
  30.8 4.1 %collective-permute-start.12 = (bf16[8,2944]{1,0:T(8,128)(2,1)S(1)}, bf16[8,2944]{1,0:T(8,128)(2,1)S(1)}, u32[]{:S(2)}, u32[]{:S(2)}) collective-permute-start(bf16[8,2944]{1,0:T(8,128)(2,1)S(1)} %get-tuple-element.34), channel_id=1, source_target_pairs={{0,4},{1,5},{2,6},{3,7},{4,0},{5,1},{6,2},{7,3},{8,12},{9,13},{10,... | collective-permute-start | bytes 141320 | tf_op jit(solution)/shard_map/ppermute | solution.py:202
  35.3 5.0 %collective-permute-start.13 = (bf16[4,5888]{1,0:T(4,128)(2,1)S(1)}, bf16[4,5888]{1,0:T(4,128)(2,1)S(1)}, u32[]{:S(2)}, u32[]{:S(2)}) collective-permute-start(bf16[4,5888]{1,0:T(4,128)(2,1)S(1)} %get-tuple-element.36), channel_id=1, source_target_pairs={{0,8},{1,9},{2,10},{3,11},{4,12},{5,13},{6,14},{7,15},{8,0},{9,1},... | collective-permute-start | bytes 141320 | tf_op jit(solution)/shard_map/ppermute | solution.py:202

commit v3 on v2

--- a/solution.py
+++ b/solution.py
@@ -77,28 +77,34 @@
                     stage((step - lag) * group + member)
 
 
-def pack_exact(values, heads):
-    lane = lax.broadcasted_iota(jnp.int32, values.shape, 1)
+def exact_terms(values):
     first = values.astype(jnp.bfloat16).astype(jnp.float32)
     rest = values - first
     second = rest.astype(jnp.bfloat16).astype(jnp.float32)
-    third = rest - second
-    tail = jnp.where(lane < 2 * heads, pltpu.roll(second, heads, 1), pltpu.roll(third, 2 * heads, 1))
-    return jnp.where(lane < heads, first, tail).astype(jnp.bfloat16)
-
-
-def unpack_exact(packed, heads):
+    return first, second, rest - second
+
+
+def pack_statistics(maxima, denominators, unit, heads):
+    lane = lax.broadcasted_iota(jnp.int32, maxima.shape, 1)
+    packed = unit
+    for place, term in enumerate((*exact_terms(maxima), *exact_terms(denominators))):
+        moved = term if place == 0 else pltpu.roll(term, place * heads, 1)
+        packed = jnp.where((lane >= place * heads) & (lane < (place + 1) * heads), moved, packed)
+    return packed.astype(jnp.bfloat16)
+
+
+def unpack_statistics(packed, heads):
     terms = packed.astype(jnp.float32)
-    return terms + (pltpu.roll(terms, HDIM - heads, 1) + pltpu.roll(terms, HDIM - 2 * heads, 1))
+    place = [terms, *(pltpu.roll(terms, HDIM - index * heads, 1) for index in range(1, 6))]
+    unit = jnp.broadcast_to(terms[:, 6 * heads : 6 * heads + 1], terms.shape)
+    return place[0] + (place[1] + place[2]), place[3] + (place[4] + place[5]), unit
 
 
 def read_statistics(ref, width, coded):
     if not coded:
         return ref[:, width : width + HDIM], ref[:, width + HDIM :], None
-    heads = width // HDIM
-    maxima = unpack_exact(ref[:, width : width + HDIM], heads)
-    denominators = unpack_exact(ref[:, width + HDIM : width + 2 * HDIM], heads)
-    return maxima, denominators, ref[:, width + 2 * HDIM :].astype(jnp.float32) * (1.0 / CODE_SPAN)
+    maxima, denominators, unit = unpack_statistics(ref[:, width:], width // HDIM)
+    return maxima, denominators, unit * (1.0 / CODE_SPAN)
 
 
 def read_numerator(ref, columns, coded):
@@ -142,7 +148,7 @@
     for chain in range(chains):
         sources = refs[2 * chain : 2 * chain + 2]
         keep_ref = section(all_keep_ref, chain, width + 2 * HDIM)
-        send_ref = section(all_send_ref, chain, width + 3 * HDIM)
+        send_ref = section(all_send_ref, chain, width + HDIM)
         maxima, denominators, factors = combine(sources, kinds, width)
         largest = jnp.full((half, HDIM), 1e-30, jnp.float32)
         for head in range(heads):
@@ -151,8 +157,9 @@
             keep_ref[:, columns] = merged[:half]
             means_ref[:, columns] = merged[half:]
             largest = jnp.maximum(largest, jnp.abs(merged[half:]))
-        units = (jnp.max(largest, axis=1, keepdims=True) * 1.01).astype(jnp.bfloat16)
-        step = jnp.broadcast_to(CODE_SPAN / units.astype(jnp.float32), largest.shape)
+        unit = jnp.broadcast_to(jnp.max(largest, axis=1, keepdims=True), largest.shape)
+        unit = (unit * 1.01).astype(jnp.bfloat16).astype(jnp.float32)
+        step = CODE_SPAN / unit
         for head in range(heads):
             columns = slice(head * HDIM, (head + 1) * HDIM)
             mean = means_ref[:, columns]
@@ -160,9 +167,7 @@
             send_ref[:, columns] = jnp.where(mean < 0, -code, code).astype(jnp.bfloat16)
         keep_ref[:, width : width + HDIM] = maxima[:half]
         keep_ref[:, width + HDIM :] = denominators[:half]
-        send_ref[:, width : width + HDIM] = pack_exact(maxima[half:], heads)
-        send_ref[:, width + HDIM : width + 2 * HDIM] = pack_exact(denominators[half:], heads)
-        send_ref[:, width + 2 * HDIM :] = jnp.broadcast_to(units, largest.shape)
+        send_ref[:, width:] = pack_statistics(maxima[half:], denominators[half:], unit, heads)
 
 
 def finish_kernel(all_here_ref, all_there_ref, gain_ref, out_ref, *, kinds, chains):
@@ -171,7 +176,7 @@
     squares = jnp.zeros((rows, HDIM), jnp.float32)
     attended = []
     for chain in range(chains):
-        sources = (section(all_here_ref, chain, width + 2 * HDIM), section(all_there_ref, chain, width + 3 * HDIM))
+        sources = (section(all_here_ref, chain, width + 2 * HDIM), section(all_there_ref, chain, width + HDIM))
         _, _, factors = combine(sources, kinds, width)
         for head in range(width // HDIM):
             block = combined_mean(sources, kinds, factors, head)
@@ -215,14 +220,16 @@
         return call(join_kernel, (shape,) * parts, [window, arrived], FETCH_FLOPS)
 
     windows = joined(queries, exchange(queries, chips[-1]), CHAINS)
-    for mask in chips[-2::-1]:
-        arrived = [exchange(w, mask) for w in windows]
+    near = chips[:-1]
+    orders = [near, near[1::-1] + near[2:]]
+    for masks in list(zip(*orders))[::-1]:
+        arrived = [exchange(w, m) for w, m in zip(windows, masks)]
         windows = [joined(w, a, 1)[0] for w, a in zip(windows, arrived)]
     arrived = [exchange(w, core) for w in windows]
     half = windows[0].shape[0]
 
     plain = lambda count, parts: jax.ShapeDtypeStruct((count, parts * (part + 2 * HDIM)), jnp.float32)
-    code = lambda count, parts: jax.ShapeDtypeStruct((count, parts * (part + 3 * HDIM)), jnp.bfloat16)
+    code = lambda count, parts: jax.ShapeDtypeStruct((count, parts * (part + HDIM)), jnp.bfloat16)
 
     def attend(chain):
         return call(
@@ -242,10 +249,10 @@
     parts = [attend(chain) for chain in range(CHAINS)]
     pairs = [(keep, exchange(send, core)) for keep, send in parts]
     kinds = ("sums", "sums")
-    for mask in chips[:-1]:
+    for masks in zip(*orders):
         half = half // 2
         parts = [merge(pair, kinds, half, 1) for pair in pairs]
-        pairs = [(keep, exchange(send, mask)) for keep, send in parts]
+        pairs = [(k, exchange(s, m)) for (k, s), m in zip(parts, masks)]
         kinds = ("means", "coded")
     keep, send = merge([array for pair in pairs for array in pair], kinds, half // 2, CHAINS)
     kernel = functools.partial(finish_kernel, kinds=("means", "coded"), chains=CHAINS)

time: 41.6 us -> 41.3 us (level)
  waiting for transfers between devices: 15.6 us -> 14.1 us
  starting transfers between devices: 17.9 us -> 19.1 us
    ppermute x14, waiting for transfers between devices: 15.6 us -> 14.1 us  [exchange(): lax.ppermute(array, 'seq', [(i, i ^ mask) for i in range(lax.axis_size('s...]
    ppermute x14, starting transfers between devices: 17.9 us -> 19.1 us  [exchange(): lax.ppermute(array, 'seq', [(i, i ^ mask) for i in range(lax.axis_size('s...]
where the time goes in v3:
time: 41.3 us; the launch traced here: 41.1 us
  starting transfers between devices  19.1 us (46%)
  waiting for transfers between devices  14.1 us (34%)
  Pallas kernels  6.93 us (17%)
  local copies, waits for them, and re-layouts  0.81 us (2%)
    ppermute x14, starting transfers between devices, exchange(): lax.ppermute(array, 'seq', [(i, i ^ mask) for i in range(lax.axis_size('s...  19.1 us
    ppermute x14, waiting for transfers between devices, exchange(): lax.ppermute(array, 'seq', [(i, i ^ mask) for i in range(lax.axis_size('s...  14.1 us
    pallas_call x14, Pallas kernels, call(): pl.pallas_call(kernel, out_shape=out_shape, in_specs=[VMEM_SPEC] * len(op...  6.93 us
  transfers between devices with their start and end apart: 14, of which 8 were waited for; matrix products, arithmetic and copies ran while one was open for 0% of the time, Pallas kernels for 13%

profile of v3, /device:TPU:0, one launch (start us, length us, event | category | flops | bytes accessed | tf_op | source)
XLA Modules:
  0.0 41.1 jit_solution(14966055713193831315)
XLA Ops:
  0.0 4.1 %collective-permute-start = (bf16[4,5120]{1,0:T(4,128)(2,1)}, bf16[4,5120]{1,0:T(4,128)(2,1)S(1)}, u32[]{:S(2)}, u32[]{:S(2)}) collective-permute-start(bf16[4,5120]{1,0:T(4,128)(2,1)} %here_ref.1), channel_id=1, source_target_pairs={{0,8},{1,9},{2,10},{3,11},{4,12},{5,13},{6,14},{7,15},{8,0},{9,1},... | collective-permute-start | bytes 122888 | tf_op jit(solution)/shard_map/ppermute | solution.py:207
  4.1 2.6 %collective-permute-done.there_ref = bf16[4,5120]{1,0:T(4,128)(2,1)S(1)} collective-permute-done((bf16[4,5120]{1,0:T(4,128)(2,1)}, bf16[4,5120]{1,0:T(4,128)(2,1)S(1)}, u32[]{:S(2)}, u32[]{:S(2)}) %collective-permute-start) | collective-permute-done | bytes 40992 | tf_op jit(solution)/shard_map/ppermute | solution.py:207
  6.7 0.8 %copy-done = bf16[4,5120]{1,0:T(4,128)(2,1)S(1)} copy-done((bf16[4,5120]{1,0:T(4,128)(2,1)S(1)}, bf16[4,5120]{1,0:T(4,128)(2,1)}, u32[]{:S(2)}) %copy-start) | copy-done | bytes 40984
  7.5 1.5 %collective-permute-start.1 = (bf16[8,2560]{1,0:T(8,128)(2,1)S(1)}, bf16[8,2560]{1,0:T(8,128)(2,1)S(1)}, u32[]{:S(2)}, u32[]{:S(2)}) collective-permute-start(bf16[8,2560]{1,0:T(8,128)(2,1)S(1)} %get-tuple-element.21.here_ref), channel_id=1, source_target_pairs={{0,4},{1,5},{2,6},{3,7},{4,0},{5,1},{6,2},{7,3},{8,12},{9,13},{10,... | collective-permute-start | bytes 122888 | tf_op jit(solution)/shard_map/ppermute | solution.py:207
  9.0 1.5 %collective-permute-start.7 = (bf16[8,2560]{1,0:T(8,128)(2,1)S(1)}, bf16[8,2560]{1,0:T(8,128)(2,1)S(1)}, u32[]{:S(2)}, u32[]{:S(2)}) collective-permute-start(bf16[8,2560]{1,0:T(8,128)(2,1)S(1)} %get-tuple-element.28.here_ref), channel_id=1, source_target_pairs={{0,2},{1,3},{2,0},{3,1},{4,6},{5,7},{6,4},{7,5},{8,10},{9,11},{10,... | collective-permute-start | bytes 122888 | tf_op jit(solution)/shard_map/ppermute | solution.py:207
  10.6 1.0 %collective-permute-done.1.there_ref = bf16[8,2560]{1,0:T(8,128)(2,1)S(1)} collective-permute-done((bf16[8,2560]{1,0:T(8,128)(2,1)S(1)}, bf16[8,2560]{1,0:T(8,128)(2,1)S(1)}, u32[]{:S(2)}, u32[]{:S(2)}) %collective-permute-start.1) | collective-permute-done | bytes 40992 | tf_op jit(solution)/shard_map/ppermute | solution.py:207
  11.6 1.8 %collective-permute-start.2 = (bf16[16,2560]{1,0:T(8,128)(2,1)S(1)}, bf16[16,2560]{1,0:T(8,128)(2,1)S(1)}, u32[]{:S(2)}, u32[]{:S(2)}) collective-permute-start(bf16[16,2560]{1,0:T(8,128)(2,1)S(1)} %shard_map.47.here_ref), channel_id=1, source_target_pairs={{0,2},{1,3},{2,0},{3,1},{4,6},{5,7},{6,4},{7,5},{8,10},{9,11},{10,... | collective-permute-start | bytes 245768 | tf_op jit(solution)/shard_map/ppermute | solution.py:207
  13.4 1.3 %collective-permute-start.8 = (bf16[16,2560]{1,0:T(8,128)(2,1)S(1)}, bf16[16,2560]{1,0:T(8,128)(2,1)S(1)}, u32[]{:S(2)}, u32[]{:S(2)}) collective-permute-start(bf16[16,2560]{1,0:T(8,128)(2,1)S(1)} %shard_map.52.here_ref), channel_id=1, source_target_pairs={{0,4},{1,5},{2,6},{3,7},{4,0},{5,1},{6,2},{7,3},{8,12},{9,13},{10,... | collective-permute-start | bytes 245768 | tf_op jit(solution)/shard_map/ppermute | solution.py:207
  14.8 1.3 %collective-permute-done.2.there_ref = bf16[16,2560]{1,0:T(8,128)(2,1)S(1)} collective-permute-done((bf16[16,2560]{1,0:T(8,128)(2,1)S(1)}, bf16[16,2560]{1,0:T(8,128)(2,1)S(1)}, u32[]{:S(2)}, u32[]{:S(2)}) %collective-permute-start.2) | collective-permute-done | bytes 81952 | tf_op jit(solution)/shard_map/ppermute | solution.py:207
  16.2 1.8 %collective-permute-done.8.there_ref = bf16[16,2560]{1,0:T(8,128)(2,1)S(1)} collective-permute-done((bf16[16,2560]{1,0:T(8,128)(2,1)S(1)}, bf16[16,2560]{1,0:T(8,128)(2,1)S(1)}, u32[]{:S(2)}, u32[]{:S(2)}) %collective-permute-start.8) | collective-permute-done | bytes 81952 | tf_op jit(solution)/shard_map/ppermute | solution.py:207
  18.1 1.9 %shard_map.49 = (f32[32,2816]{1,0:T(8,128)S(1)}, f32[32,2816]{1,0:T(8,128)S(1)}) custom-call(bf16[32,2560]{1,0:T(8,128)(2,1)S(1)} %shard_map.48.query_here_ref, bf16[32,2560]{1,0:T(8,128)(2,1)S(1)} %collective-permute-done.3.query_there_ref, bf16[512,5120]{1,0:T(8,128)(2,1)S(1)} %bitcast.2, bf16[512,5120]{1,0:T(8,128)(2,1)S(1)} %bitcast.4), custom_call_target="tpu_custom_call" | custom-call | flops 335544320 | bytes 11534336 | tf_op jit(solution)/shard_map/pallas_call | solution.py:195
  20.1 0.5 %collective-permute-start.4 = (f32[32,2816]{1,0:T(8,128)S(1)}, f32[32,2816]{1,0:T(8,128)S(1)}, u32[]{:S(2)}, u32[]{:S(2)}) collective-permute-start(f32[32,2816]{1,0:T(8,128)S(1)} %get-tuple-element.23), channel_id=1, source_target_pairs={{0,1},{1,0},{2,3},{3,2},{4,5},{5,4},{6,7},{7,6},{8,9},{9,8},{10,11... | collective-permute-start | bytes 1081352 | tf_op jit(solution)/shard_map/ppermute | solution.py:207
  20.6 1.9 %shard_map.54 = (f32[32,2816]{1,0:T(8,128)S(1)}, f32[32,2816]{1,0:T(8,128)S(1)}) custom-call(bf16[32,2560]{1,0:T(8,128)(2,1)S(1)} %shard_map.53.query_here_ref, bf16[32,2560]{1,0:T(8,128)(2,1)S(1)} %collective-permute-done.9.query_there_ref, bf16[512,5120]{1,0:T(8,128)(2,1)S(1)} %bitcast.2, bf16[512,5120]{1,0:T(8,128)(2,1)S(1)} %bitcast.4), custom_call_target="tpu_custom_call" | custom-call | flops 335544320 | bytes 11534336 | tf_op jit(solution)/shard_map/pallas_call | solution.py:195
  23.1 1.3 %collective-permute-start.5 = (bf16[16,2688]{1,0:T(8,128)(2,1)S(1)}, bf16[16,2688]{1,0:T(8,128)(2,1)S(1)}, u32[]{:S(2)}, u32[]{:S(2)}) collective-permute-start(bf16[16,2688]{1,0:T(8,128)(2,1)S(1)} %get-tuple-element.25), channel_id=1, source_target_pairs={{0,2},{1,3},{2,0},{3,1},{4,6},{5,7},{6,4},{7,5},{8,10},{9,11},{10,... | collective-permute-start | bytes 258056 | tf_op jit(solution)/shard_map/ppermute | solution.py:207
  24.8 1.3 %collective-permute-start.11 = (bf16[16,2688]{1,0:T(8,128)(2,1)S(1)}, bf16[16,2688]{1,0:T(8,128)(2,1)S(1)}, u32[]{:S(2)}, u32[]{:S(2)}) collective-permute-start(bf16[16,2688]{1,0:T(8,128)(2,1)S(1)} %get-tuple-element.32), channel_id=1, source_target_pairs={{0,4},{1,5},{2,6},{3,7},{4,0},{5,1},{6,2},{7,3},{8,12},{9,13},{10,... | collective-permute-start | bytes 258056 | tf_op jit(solution)/shard_map/ppermute | solution.py:207
  26.1 1.9 %collective-permute-done.5.refs_1_ = bf16[16,2688]{1,0:T(8,128)(2,1)S(1)} collective-permute-done((bf16[16,2688]{1,0:T(8,128)(2,1)S(1)}, bf16[16,2688]{1,0:T(8,128)(2,1)S(1)}, u32[]{:S(2)}, u32[]{:S(2)}) %collective-permute-start.5) | collective-permute-done | bytes 86048 | tf_op jit(solution)/shard_map/ppermute | solution.py:207
  28.4 1.3 %collective-permute-start.6 = (bf16[8,2688]{1,0:T(8,128)(2,1)S(1)}, bf16[8,2688]{1,0:T(8,128)(2,1)S(1)}, u32[]{:S(2)}, u32[]{:S(2)}) collective-permute-start(bf16[8,2688]{1,0:T(8,128)(2,1)S(1)} %get-tuple-element.27), channel_id=1, source_target_pairs={{0,4},{1,5},{2,6},{3,7},{4,0},{5,1},{6,2},{7,3},{8,12},{9,13},{10,... | collective-permute-start | bytes 129032 | tf_op jit(solution)/shard_map/ppermute | solution.py:207
  30.1 1.2 %collective-permute-start.12 = (bf16[8,2688]{1,0:T(8,128)(2,1)S(1)}, bf16[8,2688]{1,0:T(8,128)(2,1)S(1)}, u32[]{:S(2)}, u32[]{:S(2)}) collective-permute-start(bf16[8,2688]{1,0:T(8,128)(2,1)S(1)} %get-tuple-element.34), channel_id=1, source_target_pairs={{0,2},{1,3},{2,0},{3,1},{4,6},{5,7},{6,4},{7,5},{8,10},{9,11},{10,... | collective-permute-start | bytes 129032 | tf_op jit(solution)/shard_map/ppermute | solution.py:207
  31.3 1.2 %collective-permute-done.6.refs_1_ = bf16[8,2688]{1,0:T(8,128)(2,1)S(1)} collective-permute-done((bf16[8,2688]{1,0:T(8,128)(2,1)S(1)}, bf16[8,2688]{1,0:T(8,128)(2,1)S(1)}, u32[]{:S(2)}, u32[]{:S(2)}) %collective-permute-start.6) | collective-permute-done | bytes 43040 | tf_op jit(solution)/shard_map/ppermute | solution.py:207
  32.5 1.7 %collective-permute-done.12.refs_3_ = bf16[8,2688]{1,0:T(8,128)(2,1)S(1)} collective-permute-done((bf16[8,2688]{1,0:T(8,128)(2,1)S(1)}, bf16[8,2688]{1,0:T(8,128)(2,1)S(1)}, u32[]{:S(2)}, u32[]{:S(2)}) %collective-permute-start.12) | collective-permute-done | bytes 43040 | tf_op jit(solution)/shard_map/ppermute | solution.py:207
  34.2 0.4 shard_map.57
  34.6 3.0 %collective-permute-start.13 = (bf16[4,5376]{1,0:T(4,128)(2,1)S(1)}, bf16[4,5376]{1,0:T(4,128)(2,1)S(1)}, u32[]{:S(2)}, u32[]{:S(2)}) collective-permute-start(bf16[4,5376]{1,0:T(4,128)(2,1)S(1)} %get-tuple-element.36), channel_id=1, source_target_pairs={{0,8},{1,9},{2,10},{3,11},{4,12},{5,13},{6,14},{7,15},{8,0},{9,1},... | collective-permute-start | bytes 129032 | tf_op jit(solution)/shard_map/ppermute | solution.py:207
  37.6 2.5 %collective-permute-done.13.all_there_ref = bf16[4,5376]{1,0:T(4,128)(2,1)S(1)} collective-permute-done((bf16[4,5376]{1,0:T(4,128)(2,1)S(1)}, bf16[4,5376]{1,0:T(4,128)(2,1)S(1)}, u32[]{:S(2)}, u32[]{:S(2)}) %collective-permute-start.13) | collective-permute-done | bytes 43040 | tf_op jit(solution)/shard_map/ppermute | solution.py:207
  40.1 1.0 %shard_map.59 = bf16[4,5120]{1,0:T(4,128)(2,1)} custom-call(f32[4,5632]{1,0:T(4,128)S(1)} %get-tuple-element.35.all_here_ref, bf16[4,5376]{1,0:T(4,128)(2,1)S(1)} %collective-permute-done.13.all_there_ref, f32[1,5120]{1,0:T(1,128)S(1)} %shard_map.58.gain_ref), custom_call_target="tpu_custom_call" | custom-call | bytes 194560 | tf_op jit(solution)/shard_map/pallas_call | solution.py:195
  (32 shorter events, 1.9 us)
Async XLA Ops:
  0.0 6.7 %collective-permute-start = (bf16[4,5120]{1,0:T(4,128)(2,1)}, bf16[4,5120]{1,0:T(4,128)(2,1)S(1)}, u32[]{:S(2)}, u32[]{:S(2)}) collective-permute-start(bf16[4,5120]{1,0:T(4,128)(2,1)} %here_ref.1), channel_id=1, source_target_pairs={{0,8},{1,9},{2,10},{3,11},{4,12},{5,13},{6,14},{7,15},{8,0},{9,1},... | collective-permute-start | bytes 122888 | tf_op jit(solution)/shard_map/ppermute | solution.py:207
  6.7 0.8 %copy-start = (bf16[4,5120]{1,0:T(4,128)(2,1)S(1)}, bf16[4,5120]{1,0:T(4,128)(2,1)}, u32[]{:S(2)}) copy-start(bf16[4,5120]{1,0:T(4,128)(2,1)} %here_ref.1) | copy-start | bytes 122884
  7.5 4.1 %collective-permute-start.1 = (bf16[8,2560]{1,0:T(8,128)(2,1)S(1)}, bf16[8,2560]{1,0:T(8,128)(2,1)S(1)}, u32[]{:S(2)}, u32[]{:S(2)}) collective-permute-start(bf16[8,2560]{1,0:T(8,128)(2,1)S(1)} %get-tuple-element.21.here_ref), channel_id=1, source_target_pairs={{0,4},{1,5},{2,6},{3,7},{4,0},{5,1},{6,2},{7,3},{8,12},{9,13},{10,... | collective-permute-start | bytes 122888 | tf_op jit(solution)/shard_map/ppermute | solution.py:207
  9.0 4.3 %collective-permute-start.7 = (bf16[8,2560]{1,0:T(8,128)(2,1)S(1)}, bf16[8,2560]{1,0:T(8,128)(2,1)S(1)}, u32[]{:S(2)}, u32[]{:S(2)}) collective-permute-start(bf16[8,2560]{1,0:T(8,128)(2,1)S(1)} %get-tuple-element.28.here_ref), channel_id=1, source_target_pairs={{0,2},{1,3},{2,0},{3,1},{4,6},{5,7},{6,4},{7,5},{8,10},{9,11},{10,... | collective-permute-start | bytes 122888 | tf_op jit(solution)/shard_map/ppermute | solution.py:207
  11.6 4.5 %collective-permute-start.2 = (bf16[16,2560]{1,0:T(8,128)(2,1)S(1)}, bf16[16,2560]{1,0:T(8,128)(2,1)S(1)}, u32[]{:S(2)}, u32[]{:S(2)}) collective-permute-start(bf16[16,2560]{1,0:T(8,128)(2,1)S(1)} %shard_map.47.here_ref), channel_id=1, source_target_pairs={{0,2},{1,3},{2,0},{3,1},{4,6},{5,7},{6,4},{7,5},{8,10},{9,11},{10,... | collective-permute-start | bytes 245768 | tf_op jit(solution)/shard_map/ppermute | solution.py:207
  13.4 4.7 %slice-start = ((s8[5242880]{0:T(1024)(128)(4,1)}), s8[4194304]{0:T(1024)(128)(4,1)S(1)}, s32[]{:S(2)}) async-start(s8[5242880]{0:T(1024)(128)(4,1)} %bitcast.1), calls=%async_computation | async-start | bytes 8388608
  13.4 4.7 %slice-start.2 = ((s8[5242880]{0:T(1024)(128)(4,1)}), s8[4194304]{0:T(1024)(128)(4,1)S(1)}, s32[]{:S(2)}) async-start(s8[5242880]{0:T(1024)(128)(4,1)} %bitcast.3), calls=%async_computation.2 | async-start | bytes 8388608
  13.4 4.7 %slice-start.1 = ((s8[5242880]{0:T(1024)(128)(4,1)}), s8[1048576]{0:T(1024)(128)(4,1)S(1)}, s32[]{:S(2)}) async-start(s8[5242880]{0:T(1024)(128)(4,1)} %bitcast.1), calls=%async_computation.1 | async-start | bytes 2097152
  13.4 4.7 %slice-start.3 = ((s8[5242880]{0:T(1024)(128)(4,1)}), s8[1048576]{0:T(1024)(128)(4,1)S(1)}, s32[]{:S(2)}) async-start(s8[5242880]{0:T(1024)(128)(4,1)} %bitcast.3), calls=%async_computation.3 | async-start | bytes 2097152
  13.4 4.5 %collective-permute-start.8 = (bf16[16,2560]{1,0:T(8,128)(2,1)S(1)}, bf16[16,2560]{1,0:T(8,128)(2,1)S(1)}, u32[]{:S(2)}, u32[]{:S(2)}) collective-permute-start(bf16[16,2560]{1,0:T(8,128)(2,1)S(1)} %shard_map.52.here_ref), channel_id=1, source_target_pairs={{0,4},{1,5},{2,6},{3,7},{4,0},{5,1},{6,2},{7,3},{8,12},{9,13},{10,... | collective-permute-start | bytes 245768 | tf_op jit(solution)/shard_map/ppermute | solution.py:207
  16.1 1.9 %collective-permute-start.3 = (bf16[32,2560]{1,0:T(8,128)(2,1)S(1)}, bf16[32,2560]{1,0:T(8,128)(2,1)S(1)}, u32[]{:S(2)}, u32[]{:S(2)}) collective-permute-start(bf16[32,2560]{1,0:T(8,128)(2,1)S(1)} %shard_map.48.query_here_ref), channel_id=1, source_target_pairs={{0,1},{1,0},{2,3},{3,2},{4,5},{5,4},{6,7},{7,6},{8,9},{9,8},{10,11... | collective-permute-start | bytes 491528 | tf_op jit(solution)/shard_map/ppermute | solution.py:207
  18.0 2.7 %collective-permute-start.9 = (bf16[32,2560]{1,0:T(8,128)(2,1)S(1)}, bf16[32,2560]{1,0:T(8,128)(2,1)S(1)}, u32[]{:S(2)}, u32[]{:S(2)}) collective-permute-start(bf16[32,2560]{1,0:T(8,128)(2,1)S(1)} %shard_map.53.query_here_ref), channel_id=1, source_target_pairs={{0,1},{1,0},{2,3},{3,2},{4,5},{5,4},{6,7},{7,6},{8,9},{9,8},{10,11... | collective-permute-start | bytes 491528 | tf_op jit(solution)/shard_map/ppermute | solution.py:207
  20.1 17.6 %copy-start.1 = (f32[5120]{0:T(1024)S(1)}, f32[5120]{0:T(1024)}, u32[]{:S(2)}) copy-start(f32[5120]{0:T(1024)} %param.7) | copy-start | bytes 61444
  20.1 2.6 %collective-permute-start.4 = (f32[32,2816]{1,0:T(8,128)S(1)}, f32[32,2816]{1,0:T(8,128)S(1)}, u32[]{:S(2)}, u32[]{:S(2)}) collective-permute-start(f32[32,2816]{1,0:T(8,128)S(1)} %get-tuple-element.23), channel_id=1, source_target_pairs={{0,1},{1,0},{2,3},{3,2},{4,5},{5,4},{6,7},{7,6},{8,9},{9,8},{10,11... | collective-permute-start | bytes 1081352 | tf_op jit(solution)/shard_map/ppermute | solution.py:207
  22.6 1.8 %collective-permute-start.10 = (f32[32,2816]{1,0:T(8,128)S(1)}, f32[32,2816]{1,0:T(8,128)S(1)}, u32[]{:S(2)}, u32[]{:S(2)}) collective-permute-start(f32[32,2816]{1,0:T(8,128)S(1)} %get-tuple-element.30), channel_id=1, source_target_pairs={{0,1},{1,0},{2,3},{3,2},{4,5},{5,4},{6,7},{7,6},{8,9},{9,8},{10,11... | collective-permute-start | bytes 1081352 | tf_op jit(solution)/shard_map/ppermute | solution.py:207
  23.1 5.0 %collective-permute-start.5 = (bf16[16,2688]{1,0:T(8,128)(2,1)S(1)}, bf16[16,2688]{1,0:T(8,128)(2,1)S(1)}, u32[]{:S(2)}, u32[]{:S(2)}) collective-permute-start(bf16[16,2688]{1,0:T(8,128)(2,1)S(1)} %get-tuple-element.25), channel_id=1, source_target_pairs={{0,2},{1,3},{2,0},{3,1},{4,6},{5,7},{6,4},{7,5},{8,10},{9,11},{10,... | collective-permute-start | bytes 258056 | tf_op jit(solution)/shard_map/ppermute | solution.py:207
  24.8 5.0 %collective-permute-start.11 = (bf16[16,2688]{1,0:T(8,128)(2,1)S(1)}, bf16[16,2688]{1,0:T(8,128)(2,1)S(1)}, u32[]{:S(2)}, u32[]{:S(2)}) collective-permute-start(bf16[16,2688]{1,0:T(8,128)(2,1)S(1)} %get-tuple-element.32), channel_id=1, source_target_pairs={{0,4},{1,5},{2,6},{3,7},{4,0},{5,1},{6,2},{7,3},{8,12},{9,13},{10,... | collective-permute-start | bytes 258056 | tf_op jit(solution)/shard_map/ppermute | solution.py:207
  28.4 4.1 %collective-permute-start.6 = (bf16[8,2688]{1,0:T(8,128)(2,1)S(1)}, bf16[8,2688]{1,0:T(8,128)(2,1)S(1)}, u32[]{:S(2)}, u32[]{:S(2)}) collective-permute-start(bf16[8,2688]{1,0:T(8,128)(2,1)S(1)} %get-tuple-element.27), channel_id=1, source_target_pairs={{0,4},{1,5},{2,6},{3,7},{4,0},{5,1},{6,2},{7,3},{8,12},{9,13},{10,... | collective-permute-start | bytes 129032 | tf_op jit(solution)/shard_map/ppermute | solution.py:207
  30.1 4.1 %collective-permute-start.12 = (bf16[8,2688]{1,0:T(8,128)(2,1)S(1)}, bf16[8,2688]{1,0:T(8,128)(2,1)S(1)}, u32[]{:S(2)}, u32[]{:S(2)}) collective-permute-start(bf16[8,2688]{1,0:T(8,128)(2,1)S(1)} %get-tuple-element.34), channel_id=1, source_target_pairs={{0,2},{1,3},{2,0},{3,1},{4,6},{5,7},{6,4},{7,5},{8,10},{9,11},{10,... | collective-permute-start | bytes 129032 | tf_op jit(solution)/shard_map/ppermute | solution.py:207
  34.6 5.5 %collective-permute-start.13 = (bf16[4,5376]{1,0:T(4,128)(2,1)S(1)}, bf16[4,5376]{1,0:T(4,128)(2,1)S(1)}, u32[]{:S(2)}, u32[]{:S(2)}) collective-permute-start(bf16[4,5376]{1,0:T(4,128)(2,1)S(1)} %get-tuple-element.36), channel_id=1, source_target_pairs={{0,8},{1,9},{2,10},{3,11},{4,12},{5,13},{6,14},{7,15},{8,0},{9,1},... | collective-permute-start | bytes 129032 | tf_op jit(solution)/shard_map/ppermute | solution.py:207
